TPU v7x, 512 devices: a whole 4x4x16 slice. The times are simulated.
512 devices in a mesh: pipe: 4 (over z_hi), ctx: 32 (over x, y, core), chan: 4 (over z_lo).
Axes of the slice: x: 4, y: 4, z: 16 (z_hi: 4, z_lo: 4; z = z_hi * 4 + z_lo), core: 2. Of those that a mesh axis runs over, the one named last changes fastest.
Arguments:
- handed_back: bfloat16 [4, 1, 4096, 4096], P('pipe', None, 'chan', 'ctx'), may hold values from -6 to 6
- gate_q: bfloat16 [4, 1, 4096, 4096], P('pipe', None, 'chan', 'ctx'), may hold values from -6 to 6
- key_k: bfloat16 [4, 1, 4096, 4096], P('pipe', None, 'chan', 'ctx'), may hold values from -6 to 6
- input_x: bfloat16 [4, 1, 4096, 4096], P('pipe', None, 'chan', 'ctx'), may hold values from -6 to 6
- filter_h: bfloat16 [4, 4096, 4096], P('pipe', 'chan', 'ctx'), may hold values from -1.5 to 1.5
- doc_lengths: int32 [1, 8], replicated, may hold values from 1 to 1024, 4096 in all within a row
- section_layers: int32 [4], replicated, may hold values from 2 to 12
Outputs:
- grad_input: bfloat16 [4, 1, 4096, 4096], P('pipe', None, 'chan', 'ctx')
- grad_gate: bfloat16 [4, 1, 4096, 4096], P('pipe', None, 'chan', 'ctx')
- grad_key: bfloat16 [4, 1, 4096, 4096], P('pipe', None, 'chan', 'ctx')
- grad_filter: float32 [4, 4096, 4096], P('pipe', 'chan', 'ctx')
Inputs may be any that keep to these rules, and one draw needn't show every extreme that they name: `doc_lengths`: positions from 4096 minus a row's last entry onward are padding.
All inputs are finite; a program needn't handle non-finite values.
Results may differ from a plain program's by a relative error of at most 0.0085.
Values may be sent and summed in bfloat16 or wider, within the bound.
A program may use at most 64 MiB of HBM per device.

v0:
```python
import functools
import math

import jax
import jax.numpy as jnp
import numpy as np
from jax import lax
from jax.experimental import pallas as pl
from jax.experimental.pallas import tpu as pltpu
from jax.sharding import PartitionSpec as P

GROUP = 8


def halves(table):
    top = table.astype(jnp.bfloat16)
    rest = (table - top.astype(np.float64)).astype(jnp.bfloat16)
    return np.stack([top, rest])


@functools.lru_cache(maxsize=None)
def tables(blocks, width):
    length = blocks * width
    turn = 2.0 * math.pi
    row = np.arange(blocks)[:, None]
    quarter = np.arange(blocks)[:, None] + 0.25
    outer = turn * quarter * row.T / blocks
    wave = np.concatenate([np.cos(outer), -np.sin(outer)])
    spread = np.kron(wave, np.eye(GROUP))
    twist = np.repeat(turn * quarter * np.arange(width)[None, :] / length, GROUP, axis=0)
    lane = np.arange(width)
    inner = turn * ((lane[:, None] * lane[None, :]) % width) / width
    cos, sin = np.cos(inner), np.sin(inner)
    ahead = np.block([[cos, -sin], [sin, cos]])
    back = np.block([[cos, sin], [-sin, cos]])
    turns = np.stack([np.cos(twist), -np.sin(twist)]).astype(np.float32)
    return (halves(spread), halves(spread.T / length), halves(ahead), halves(back), turns)


def fixed_left(table_ref, right):
    return jnp.dot(table_ref[0], right, preferred_element_type=jnp.float32) + jnp.dot(
        table_ref[1], right, preferred_element_type=jnp.float32
    )


def fixed_right(left, table_ref):
    return jnp.dot(left, table_ref[0], preferred_element_type=jnp.float32) + jnp.dot(
        left, table_ref[1], preferred_element_type=jnp.float32
    )


def transform(wide_ref, spec_ref, spread_ref, ahead_ref, turns_ref):
    blocks, channels, width = wide_ref.shape
    rows = blocks * GROUP
    for pair in range(channels // (2 * GROUP)):
        chunk = wide_ref[:, 2 * GROUP * pair : 2 * GROUP * (pair + 1), :].astype(jnp.float32)
        sides = [chunk[:, :GROUP, :].reshape(rows, width), chunk[:, GROUP:, :].reshape(rows, width)]
        mixed = fixed_left(spread_ref, jnp.concatenate(sides, axis=1).astype(jnp.bfloat16))
        for side in range(2):
            part = mixed[:, side * width : (side + 1) * width]
            part_re, part_im = part[:rows], part[rows:]
            turned = jnp.concatenate(
                [
                    part_re * turns_ref[0] - part_im * turns_ref[1],
                    part_re * turns_ref[1] + part_im * turns_ref[0],
                ],
                axis=1,
            )
            spec_ref[2 * pair + side] = fixed_right(turned.astype(jnp.bfloat16), ahead_ref)


def multiply(left_ref, right_ref, conjugate, wide_ref, gather_ref, back_ref, turns_ref):
    blocks, channels, width = wide_ref.shape
    rows = blocks * GROUP
    for pair in range(channels // (2 * GROUP)):
        sides = []
        for side in range(2):
            left, right = left_ref[2 * pair + side], right_ref[2 * pair + side]
            left_re, left_im = left[:, :width], left[:, width:]
            right_re, right_im = right[:, :width], right[:, width:]
            if conjugate:
                left_im = -left_im
            both = jnp.concatenate(
                [left_re * right_re - left_im * right_im, left_re * right_im + left_im * right_re],
                axis=1,
            )
            part = fixed_right(both.astype(jnp.bfloat16), back_ref)
            part_re, part_im = part[:, :width], part[:, width:]
            sides.append(
                jnp.concatenate(
                    [
                        part_re * turns_ref[0] + part_im * turns_ref[1],
                        part_im * turns_ref[0] - part_re * turns_ref[1],
                    ],
                    axis=0,
                )
            )
        signal = fixed_left(gather_ref, jnp.concatenate(sides, axis=1).astype(jnp.bfloat16))
        outs = [signal[:, s * width : (s + 1) * width].reshape(blocks, GROUP, width) for s in range(2)]
        chunk = jnp.concatenate(outs, axis=1).astype(jnp.bfloat16)
        wide_ref[:, 2 * GROUP * pair : 2 * GROUP * (pair + 1), :] = chunk


def kernel(
    filter_ref, prod_ref, grad_ref, spread_ref, gather_ref, ahead_ref, back_ref, turns_ref,
    conv_ref, corr_ref, lag_ref, filter_spec, prod_spec, grad_spec,
):
    transform(filter_ref, filter_spec, spread_ref, ahead_ref, turns_ref)
    transform(prod_ref, prod_spec, spread_ref, ahead_ref, turns_ref)
    transform(grad_ref, grad_spec, spread_ref, ahead_ref, turns_ref)
    multiply(filter_spec, prod_spec, False, conv_ref, gather_ref, back_ref, turns_ref)
    multiply(filter_spec, grad_spec, True, corr_ref, gather_ref, back_ref, turns_ref)
    multiply(prod_spec, grad_spec, True, lag_ref, gather_ref, back_ref, turns_ref)


def spectra(filter_wide, prod_wide, grad_wide):
    blocks, channels, width = filter_wide.shape
    out = jax.ShapeDtypeStruct((blocks, channels, width), jnp.bfloat16)
    spec = pltpu.VMEM((channels // GROUP, blocks * GROUP, 2 * width), jnp.float32)
    held = pl.BlockSpec(memory_space=pltpu.VMEM)
    return pl.pallas_call(
        kernel,
        out_shape=(out, out, out),
        in_specs=[held] * 8,
        out_specs=(held, held, held),
        scratch_shapes=[spec, spec, spec],
        compiler_params=pltpu.CompilerParams(vmem_limit_bytes=48 * 1024 * 1024),
    )(filter_wide, prod_wide, grad_wide, *tables(blocks, width))


def exchange(value):
    return lax.all_to_all(value, "ctx", split_axis=0, concat_axis=0, tiled=True)


def body(handed_back, gate_q, key_k, input_x, filter_h, doc_lengths, section_layers):
    channels, width = gate_q.shape[2:]
    blocks = lax.axis_size("ctx")
    pipe = lax.axis_size("pipe")
    length = blocks * width
    shape = (blocks, channels // blocks, width)
    layers = section_layers[lax.axis_index("pipe")]
    scale = 1.0 / jnp.sqrt(layers.astype(jnp.float32))
    spots = lax.axis_index("ctx") * width + jnp.arange(width, dtype=jnp.int32)
    live = (spots < length - doc_lengths[0, -1]).astype(jnp.float32)
    incoming = lax.ppermute(handed_back, "pipe", [(s, (s - 1) % pipe) for s in range(pipe)])
    key32 = key_k.reshape(shape).astype(jnp.float32)
    input32 = input_x.reshape(shape).astype(jnp.float32)
    product = (key32 * input32 * live).astype(jnp.bfloat16)
    first = exchange(jnp.stack([product, filter_h.reshape(shape)], axis=1))
    grad32 = incoming.reshape(shape).astype(jnp.float32)
    gate32 = gate_q.reshape(shape).astype(jnp.float32)
    branch = exchange((scale * gate32 * grad32).astype(jnp.bfloat16))
    results = spectra(first[:, 1], first[:, 0], branch)
    home = exchange(jnp.stack(results, axis=1)).astype(jnp.float32)
    conv32, corr32, lags = home[:, 0], home[:, 1], home[:, 2]
    grad_gate = (scale * grad32 * conv32).astype(jnp.bfloat16)
    grad_key = (corr32 * input32 * live).astype(jnp.bfloat16)
    grad_input = (grad32 + corr32 * key32 * live).astype(jnp.bfloat16)
    grad_filter = lags / math.sqrt(length)
    flat = gate_q.shape
    return (
        grad_input.reshape(flat),
        grad_gate.reshape(flat),
        grad_key.reshape(flat),
        grad_filter.reshape(filter_h.shape),
    )


def solution(mesh):
    return jax.shard_map(
        body,
        mesh=mesh,
        in_specs=(
            P("pipe", None, "chan", "ctx"),
            P("pipe", None, "chan", "ctx"),
            P("pipe", None, "chan", "ctx"),
            P("pipe", None, "chan", "ctx"),
            P("pipe", "chan", "ctx"),
            P(),
            P(),
        ),
        out_specs=(
            P("pipe", None, "chan", "ctx"),
            P("pipe", None, "chan", "ctx"),
            P("pipe", None, "chan", "ctx"),
            P("pipe", "chan", "ctx"),
        ),
        check_vma=False,
    )
```

profile of v0, /device:TPU:1, one launch (start us, length us, event | category | flops | bytes accessed | tf_op | source)
XLA Modules:
  0.0 90.4 jit_solution(10324128501937022218)
XLA Ops:
  0.6 0.0 copy-start.7
  0.6 1.3 %slice.18 = s32[1,1]{1,0:T(1,128)} slice(s32[1,8]{1,0:T(1,128)} %param.17), slice={[0:1], [7:8]} | slice | bytes 8 | tf_op jit(solution)/shard_map/slice | solution.py:144
  2.6 1.1 %convert_multiply_fusion.3 = f32[1,1,1024,128]{3,2,1,0:T(8,128)S(1)} fusion(bf16[1,1,1024,128]{3,2,1,0:T(8,128)(2,1)} %param.15, bf16[1,1,1024,128]{3,2,1,0:T(8,128)(2,1)} %param.14), kind=kLoop, calls=%fused_computation.5 | loop fusion | flops 393216 | bytes 1048576 | tf_op jit(solution)/shard_map/mul | solution.py:148
  3.7 0.0 copy-start.9
  3.7 0.0 copy-start.10
  3.7 0.0 copy-start.8
  3.8 0.0 copy-done.7
  3.8 0.8 pad_maximum_fusion.1
  4.6 0.0 copy-start
  4.6 0.0 copy-start.1
  4.6 0.0 copy-start.2
  4.6 0.0 copy-start.3
  4.6 0.0 copy-start.4
  4.6 10.5 %all-to-all-start = ((bf16[32,2,32,128]{3,2,1,0:T(8,128)(2,1)}), bf16[32,2,32,128]{3,2,1,0:T(8,128)(2,1)S(1)}, u32[]{:S(2)}, u32[]{:S(2)}) async-start(bf16[32,2,32,128]{3,2,1,0:T(8,128)(2,1)} %pad_maximum_fusion.1), calls=%async_computation | async-start | bytes 1048576 | tf_op jit(solution)/shard_map/all_to_all | solution.py:132
  15.2 0.0 copy-done.9
  15.2 10.7 %collective-permute-start = (bf16[1,1,1024,128]{3,2,1,0:T(8,128)(2,1)S(1)}, bf16[1,1,1024,128]{3,2,1,0:T(8,128)(2,1)S(1)}, u32[]{:S(2)}, u32[]{:S(2)}) collective-permute-start(bf16[1,1,1024,128]{3,2,1,0:T(8,128)(2,1)S(1)} %copy-done.9), channel_id=1, source_target_pairs={{0,384},{128,0},{256,128},{384,256},{1,385},{129,1},{257,129},{385... | collective-permute-start | bytes 786440 | tf_op jit(solution)/shard_map/ppermute | solution.py:145
  25.9 0.0 copy-done.10
  25.9 0.6 dynamic_slice.3
  27.1 18.4 %collective-permute-done = bf16[1,1,1024,128]{3,2,1,0:T(8,128)(2,1)S(1)} collective-permute-done((bf16[1,1,1024,128]{3,2,1,0:T(8,128)(2,1)S(1)}, bf16[1,1,1024,128]{3,2,1,0:T(8,128)(2,1)S(1)}, u32[]{:S(2)}, u32[]{:S(2)}) %collective-permute-start) | collective-permute-done | bytes 262176 | tf_op jit(solution)/shard_map/ppermute | solution.py:145
  45.5 0.0 copy-done.8
  45.5 0.8 fusion.3
  46.3 0.0 all-to-all-done
  46.3 10.7 %all-to-all-start.1 = ((bf16[32,32,128]{2,1,0:T(8,128)(2,1)}), bf16[32,32,128]{2,1,0:T(8,128)(2,1)S(1)}, u32[]{:S(2)}, u32[]{:S(2)}) async-start(bf16[32,32,128]{2,1,0:T(8,128)(2,1)} %bitcast.6), calls=%async_computation.1 | async-start | bytes 524288 | tf_op jit(solution)/shard_map/all_to_all | solution.py:132
  57.1 8.9 %all-to-all-done.1.grad_ref = bf16[32,32,128]{2,1,0:T(8,128)(2,1)S(1)} async-done(((bf16[32,32,128]{2,1,0:T(8,128)(2,1)}), bf16[32,32,128]{2,1,0:T(8,128)(2,1)S(1)}, u32[]{:S(2)}, u32[]{:S(2)}) %all-to-all-start.1) | async-done | bytes 262176 | tf_op jit(solution)/shard_map/all_to_all | solution.py:132
  66.0 0.0 copy-done
  66.0 0.0 copy-done.1
  66.0 0.0 copy-done.2
  66.1 0.0 copy-done.3
  66.1 0.0 copy-done.4
  66.1 3.9 %shard_map.147 = (bf16[32,32,128]{2,1,0:T(8,128)(2,1)S(1)}, bf16[32,32,128]{2,1,0:T(8,128)(2,1)S(1)}, bf16[32,32,128]{2,1,0:T(8,128)(2,1)S(1)}) custom-call(bf16[32,32,128]{2,1,0:T(8,128)(2,1)S(1)} %get-tuple-element.15.filter_ref, bf16[32,32,128]{2,1,0:T(8,128)(2,1)S(1)} %get-tuple-element.14.prod_ref, bf16[32,32,128]{2,1,0:T(8,128)(2,1)S(1)} %all-to-all-done.1.grad_ref, ...), custom_call_target="tpu_custom_call" | custom-call | tf_op jit(solution)/shard_map/pallas_call | solution.py:121
  70.0 0.1 pad_maximum_fusion
  70.1 0.1 copy.18
  70.2 17.7 %all_to_all.15 = bf16[32,3,32,128]{3,2,1,0:T(8,128)(2,1)S(1)} all-to-all(bf16[32,3,32,128]{3,2,1,0:T(8,128)(2,1)S(1)} %copy.18), channel_id=1, replica_groups=mesh['pipe'=4,'ctx'=32,'chan'=4] {'ctx'}, dimensions={0} | all-to-all | bytes 1572864 | tf_op jit(solution)/shard_map/all_to_all | solution.py:132
  87.9 0.2 convert_element_type.85
  88.1 0.0 copy-start.5
  88.1 0.0 copy-start.6
  88.1 0.8 slice_multiply_fusion
  88.9 0.1 fusion.7
  89.1 0.0 copy-done.5
  89.1 0.2 copy-done.6
  89.3 1.0 %fusion.2 = (bf16[1,1,1024,128]{3,2,1,0:T(8,128)(2,1)}, bf16[1,1,1024,128]{3,2,1,0:T(8,128)(2,1)}, bf16[1,1,1024,128]{3,2,1,0:T(8,128)(2,1)}) fusion(f32[1,1,1024,128]{3,2,1,0:T(8,128)S(1)} %bitcast.23, bf16[1,1,1024,128]{3,2,1,0:T(8,128)(2,1)S(1)} %copy-done.5, f32[128]{0:T(128)S(1)} %compare_convert_fusion, bf16[1,1,1024,128]{3,2,1,0:T(8,128)(2,1)S(1)} %copy-done.6, ...), kind=kLoop, calls=%fused_computation.9 | loop fusion | flops 1703936 | bytes 2621956 | tf_op jit(solution)/shard_map/convert_element_type | solution.py:157
  (3 shorter events, 0.1 us)
Async XLA Ops:
  0.6 3.1 %copy-start.7 = (bf16[1,1024,128]{2,1,0:T(8,128)(2,1)S(1)}, bf16[1,1024,128]{2,1,0:T(8,128)(2,1)}, u32[]{:S(2)}) copy-start(bf16[1,1024,128]{2,1,0:T(8,128)(2,1)} %param.16) | copy-start | bytes 786436
  3.7 11.5 %copy-start.9 = (bf16[1,1,1024,128]{3,2,1,0:T(8,128)(2,1)S(1)}, bf16[1,1,1024,128]{3,2,1,0:T(8,128)(2,1)}, u32[]{:S(2)}) copy-start(bf16[1,1,1024,128]{3,2,1,0:T(8,128)(2,1)} %param.12) | copy-start | bytes 786436
  3.7 22.2 %copy-start.10 = (s32[4]{0:T(128)S(1)}, s32[4]{0:T(128)}, u32[]{:S(2)}) copy-start(s32[4]{0:T(128)} %param.18) | copy-start | bytes 52
  3.7 41.8 %copy-start.8 = (bf16[1,1,1024,128]{3,2,1,0:T(8,128)(2,1)S(1)}, bf16[1,1,1024,128]{3,2,1,0:T(8,128)(2,1)}, u32[]{:S(2)}) copy-start(bf16[1,1,1024,128]{3,2,1,0:T(8,128)(2,1)} %param.13) | copy-start | bytes 786436
  4.6 61.4 %copy-start = (bf16[2,256,512]{2,1,0:T(8,128)(2,1)S(1)}, bf16[2,256,512]{2,1,0:T(8,128)(2,1)}, u32[]{:S(2)}) copy-start(bf16[2,256,512]{2,1,0:T(8,128)(2,1)} %constant.35.clone.gather_ref) | copy-start | bytes 1572868
  4.6 61.4 %copy-start.1 = (bf16[2,512,256]{2,1,0:T(8,128)(2,1)S(1)}, bf16[2,512,256]{2,1,0:T(8,128)(2,1)}, u32[]{:S(2)}) copy-start(bf16[2,512,256]{2,1,0:T(8,128)(2,1)} %constant.34.clone.spread_ref) | copy-start | bytes 1572868
  4.6 61.4 %copy-start.2 = (f32[2,256,128]{2,1,0:T(8,128)S(1)}, f32[2,256,128]{2,1,0:T(8,128)}, u32[]{:S(2)}) copy-start(f32[2,256,128]{2,1,0:T(8,128)} %constant.38.clone.turns_ref) | copy-start | bytes 786436
  4.6 61.4 %copy-start.3 = (bf16[2,256,256]{2,1,0:T(8,128)(2,1)S(1)}, bf16[2,256,256]{2,1,0:T(8,128)(2,1)}, u32[]{:S(2)}) copy-start(bf16[2,256,256]{2,1,0:T(8,128)(2,1)} %constant.37.clone.back_ref) | copy-start | bytes 786436
  4.6 61.4 %copy-start.4 = (bf16[2,256,256]{2,1,0:T(8,128)(2,1)S(1)}, bf16[2,256,256]{2,1,0:T(8,128)(2,1)}, u32[]{:S(2)}) copy-start(bf16[2,256,256]{2,1,0:T(8,128)(2,1)} %constant.36.clone.ahead_ref) | copy-start | bytes 786436
  4.6 41.7 %all-to-all-start = ((bf16[32,2,32,128]{3,2,1,0:T(8,128)(2,1)}), bf16[32,2,32,128]{3,2,1,0:T(8,128)(2,1)S(1)}, u32[]{:S(2)}, u32[]{:S(2)}) async-start(bf16[32,2,32,128]{3,2,1,0:T(8,128)(2,1)} %pad_maximum_fusion.1), calls=%async_computation | async-start | bytes 1048576 | tf_op jit(solution)/shard_map/all_to_all | solution.py:132
  15.2 30.3 %collective-permute-start = (bf16[1,1,1024,128]{3,2,1,0:T(8,128)(2,1)S(1)}, bf16[1,1,1024,128]{3,2,1,0:T(8,128)(2,1)S(1)}, u32[]{:S(2)}, u32[]{:S(2)}) collective-permute-start(bf16[1,1,1024,128]{3,2,1,0:T(8,128)(2,1)S(1)} %copy-done.9), channel_id=1, source_target_pairs={{0,384},{128,0},{256,128},{384,256},{1,385},{129,1},{257,129},{385... | collective-permute-start | bytes 786440 | tf_op jit(solution)/shard_map/ppermute | solution.py:145
  46.3 19.7 %all-to-all-start.1 = ((bf16[32,32,128]{2,1,0:T(8,128)(2,1)}), bf16[32,32,128]{2,1,0:T(8,128)(2,1)S(1)}, u32[]{:S(2)}, u32[]{:S(2)}) async-start(bf16[32,32,128]{2,1,0:T(8,128)(2,1)} %bitcast.6), calls=%async_computation.1 | async-start | bytes 524288 | tf_op jit(solution)/shard_map/all_to_all | solution.py:132
  88.1 1.0 %copy-start.5 = (bf16[1,1,1024,128]{3,2,1,0:T(8,128)(2,1)S(1)}, bf16[1,1,1024,128]{3,2,1,0:T(8,128)(2,1)}, u32[]{:S(2)}) copy-start(bf16[1,1,1024,128]{3,2,1,0:T(8,128)(2,1)} %param.15) | copy-start | bytes 786436
  88.1 1.2 %copy-start.6 = (bf16[1,1,1024,128]{3,2,1,0:T(8,128)(2,1)S(1)}, bf16[1,1,1024,128]{3,2,1,0:T(8,128)(2,1)}, u32[]{:S(2)}) copy-start(bf16[1,1,1024,128]{3,2,1,0:T(8,128)(2,1)} %param.14) | copy-start | bytes 786436
where the time goes:
time: 90.8 us; the launch traced here: 90.4 us
  starting transfers between devices  31.9 us (35%)
  waiting for transfers between devices  27.3 us (30%)
  blocking collectives  17.7 us (19%)
  other arithmetic  4.95 us (5%)
  Pallas kernels  3.92 us (4%)
  local copies, waits for them, and re-layouts  2.36 us (3%)
  between operations  2.19 us (2%)
    all_to_all x2, starting transfers between devices, exchange(): return lax.all_to_all(value, 'ctx', split_axis=0, concat_axis=0, tiled=True)  21.3 us
    ppermute x1, waiting for transfers between devices, body(): lax.ppermute(handed_back, 'pipe', [(s, (s - 1) % pipe) for s in range(pip...  18.4 us
    all_to_all x1, blocking collectives, exchange(): return lax.all_to_all(value, 'ctx', split_axis=0, concat_axis=0, tiled=True)  17.7 us
    ppermute x1, starting transfers between devices, body(): lax.ppermute(handed_back, 'pipe', [(s, (s - 1) % pipe) for s in range(pip...  10.7 us
    all_to_all x2, waiting for transfers between devices, exchange(): return lax.all_to_all(value, 'ctx', split_axis=0, concat_axis=0, tiled=True)  8.92 us
    pallas_call x1, Pallas kernels, spectra(): pl.pallas_call(kernel, out_shape=(out, out, out), in_specs=[held] * 8, ou...  3.92 us
  transfers between devices with their start and end apart: 3, of which 2 were waited for; matrix products, arithmetic and copies ran while one was open for 2% of the time, Pallas kernels for 0%

commit v1 on v0

--- a/solution.py
+++ b/solution.py
@@ -49,10 +49,10 @@
     )
 
 
-def transform(wide_ref, spec_ref, spread_ref, ahead_ref, turns_ref):
+def transform(wide_ref, spec_ref, pairs, spread_ref, ahead_ref, turns_ref):
     blocks, channels, width = wide_ref.shape
     rows = blocks * GROUP
-    for pair in range(channels // (2 * GROUP)):
+    for pair in pairs:
         chunk = wide_ref[:, 2 * GROUP * pair : 2 * GROUP * (pair + 1), :].astype(jnp.float32)
         sides = [chunk[:, :GROUP, :].reshape(rows, width), chunk[:, GROUP:, :].reshape(rows, width)]
         mixed = fixed_left(spread_ref, jnp.concatenate(sides, axis=1).astype(jnp.bfloat16))
@@ -69,10 +69,10 @@
             spec_ref[2 * pair + side] = fixed_right(turned.astype(jnp.bfloat16), ahead_ref)
 
 
-def multiply(left_ref, right_ref, conjugate, wide_ref, gather_ref, back_ref, turns_ref):
+def multiply(left_ref, right_ref, conjugate, wide_ref, pairs, gather_ref, back_ref, turns_ref):
     blocks, channels, width = wide_ref.shape
     rows = blocks * GROUP
-    for pair in range(channels // (2 * GROUP)):
+    for pair in pairs:
         sides = []
         for side in range(2):
             left, right = left_ref[2 * pair + side], right_ref[2 * pair + side]
@@ -100,63 +100,175 @@
         chunk = jnp.concatenate(outs, axis=1).astype(jnp.bfloat16)
         wide_ref[:, 2 * GROUP * pair : 2 * GROUP * (pair + 1), :] = chunk
 
+MESH = pl.DeviceIdType.MESH
+FILTER, PRODUCT, CONV, GRAD, CORR, LAG = 0, 1, 2, 3, 5, 7
+STREAMS = 9
+
 
 def kernel(
-    filter_ref, prod_ref, grad_ref, spread_ref, gather_ref, ahead_ref, back_ref, turns_ref,
-    conv_ref, corr_ref, lag_ref, filter_spec, prod_spec, grad_spec,
+    docs_ref, layers_ref, handed_ref, gate_ref, key_ref, input_ref, filter_ref,
+    spread_ref, gather_ref, ahead_ref, back_ref, turns_ref,
+    incoming_ref, conv_ref, corr_ref, lag_ref, live_ref, scale_ref,
+    prod_out, grad_out, filter_wide, prod_wide, grad_wide, conv_wide, corr_wide, lag_wide,
+    filter_spec, prod_spec, grad_spec,
+    send_sems, recv_sems, relay_send, relay_recv,
 ):
-    transform(filter_ref, filter_spec, spread_ref, ahead_ref, turns_ref)
-    transform(prod_ref, prod_spec, spread_ref, ahead_ref, turns_ref)
-    transform(grad_ref, grad_spec, spread_ref, ahead_ref, turns_ref)
-    multiply(filter_spec, prod_spec, False, conv_ref, gather_ref, back_ref, turns_ref)
-    multiply(filter_spec, grad_spec, True, corr_ref, gather_ref, back_ref, turns_ref)
-    multiply(prod_spec, grad_spec, True, lag_ref, gather_ref, back_ref, turns_ref)
-
-
-def spectra(filter_wide, prod_wide, grad_wide):
-    blocks, channels, width = filter_wide.shape
-    out = jax.ShapeDtypeStruct((blocks, channels, width), jnp.bfloat16)
+    blocks, channels, width = key_ref.shape
+    me = lax.axis_index("ctx")
+    section, sections = lax.axis_index("pipe"), lax.axis_size("pipe")
+    before = lax.rem(section + sections - 1, sections)
+    after = lax.rem(section + 1, sections)
+    pairs = channels // (2 * GROUP)
+    whole = pl.ds(0, channels)
+
+    def part(pair):
+        return pl.ds(2 * GROUP * pair, 2 * GROUP)
+
+    def relay(pair):
+        return pltpu.make_async_remote_copy(
+            src_ref=handed_ref.at[:, part(pair), :],
+            dst_ref=incoming_ref.at[:, part(pair), :],
+            send_sem=relay_send.at[pair],
+            recv_sem=relay_recv.at[pair],
+            device_id={"pipe": before},
+            device_id_type=MESH,
+        )
+
+    def scatter(source, target, span, stream):
+        def step(index, carry):
+            peer = lax.rem(me + index, blocks)
+            pltpu.make_async_remote_copy(
+                src_ref=source.at[peer, span, :],
+                dst_ref=target.at[me, span, :],
+                send_sem=send_sems.at[stream],
+                recv_sem=recv_sems.at[stream],
+                device_id={"ctx": peer},
+                device_id_type=MESH,
+            ).start()
+            return carry
+
+        lax.fori_loop(1, blocks, step, 0)
+        target[me, span, :] = source[me, span, :]
+
+    def settle(buffer, span, stream):
+        others = buffer.at[pl.ds(0, blocks - 1), span, :]
+        return pltpu.make_async_remote_copy(
+            src_ref=others,
+            dst_ref=others,
+            send_sem=send_sems.at[stream],
+            recv_sem=recv_sems.at[stream],
+            device_id={"ctx": lax.rem(me + 1, blocks)},
+            device_id_type=MESH,
+        )
+
+    barrier = pltpu.get_barrier_semaphore()
+
+    def greet(index, carry):
+        pl.semaphore_signal(
+            barrier, inc=1, device_id={"ctx": lax.rem(me + index, blocks)}, device_id_type=MESH
+        )
+        return carry
+
+    for neighbour in (before, after):
+        pl.semaphore_signal(barrier, inc=1, device_id={"pipe": neighbour}, device_id_type=MESH)
+    lax.fori_loop(1, blocks, greet, 0)
+
+    spots = me * width + lax.broadcasted_iota(jnp.int32, live_ref.shape, 1)
+    limit = blocks * width - docs_ref[0, docs_ref.shape[1] - 1]
+    live_ref[...] = (spots < limit).astype(jnp.float32)
+    layers = jnp.full(scale_ref.shape, layers_ref[section], jnp.int32)
+    scale_ref[...] = 1.0 / jnp.sqrt(layers.astype(jnp.float32))
+    live = live_ref[:1, :][None]
+    scale = scale_ref[:1, :][None]
+    prod_out[...] = (
+        key_ref[...].astype(jnp.float32) * input_ref[...].astype(jnp.float32) * live
+    ).astype(jnp.bfloat16)
+    pl.semaphore_wait(barrier, blocks + 1)
+
+    for pair in range(pairs):
+        relay(pair).start()
+    scatter(filter_ref, filter_wide, whole, FILTER)
+    scatter(prod_out, prod_wide, whole, PRODUCT)
+    settle(filter_wide, whole, FILTER).wait_recv()
+    transform(filter_wide, filter_spec, range(pairs), spread_ref, ahead_ref, turns_ref)
+    settle(prod_wide, whole, PRODUCT).wait_recv()
+    transform(prod_wide, prod_spec, range(pairs), spread_ref, ahead_ref, turns_ref)
+    multiply(
+        filter_spec, prod_spec, False, conv_wide, range(pairs), gather_ref, back_ref, turns_ref
+    )
+    scatter(conv_wide, conv_ref, whole, CONV)
+
+    for pair in range(pairs):
+        span = part(pair)
+        relay(pair).wait_recv()
+        grad_out[:, span, :] = (
+            scale
+            * gate_ref[:, span, :].astype(jnp.float32)
+            * incoming_ref[:, span, :].astype(jnp.float32)
+        ).astype(jnp.bfloat16)
+        scatter(grad_out, grad_wide, span, GRAD + pair)
+        settle(grad_wide, span, GRAD + pair).wait_recv()
+        transform(grad_wide, grad_spec, [pair], spread_ref, ahead_ref, turns_ref)
+        multiply(
+            filter_spec, grad_spec, True, corr_wide, [pair], gather_ref, back_ref, turns_ref
+        )
+        scatter(corr_wide, corr_ref, span, CORR + pair)
+        multiply(prod_spec, grad_spec, True, lag_wide, [pair], gather_ref, back_ref, turns_ref)
+        scatter(lag_wide, lag_ref, span, LAG + pair)
+
+    settle(conv_ref, whole, CONV).wait_recv()
+    settle(filter_wide, whole, FILTER).wait_send()
+    settle(prod_wide, whole, PRODUCT).wait_send()
+    settle(conv_ref, whole, CONV).wait_send()
+    for pair in range(pairs):
+        relay(pair).wait_send()
+        settle(grad_wide, part(pair), GRAD + pair).wait_send()
+        settle(corr_ref, part(pair), CORR + pair).wait()
+        settle(lag_ref, part(pair), LAG + pair).wait()
+
+
+def mixer(docs, layers, handed, gate, key, inputs, filters):
+    blocks, channels, width = key.shape
+    moved = jax.ShapeDtypeStruct(key.shape, jnp.bfloat16)
+    line = jax.ShapeDtypeStruct((8, width), jnp.float32)
+    wide = pltpu.VMEM(key.shape, jnp.bfloat16)
     spec = pltpu.VMEM((channels // GROUP, blocks * GROUP, 2 * width), jnp.float32)
     held = pl.BlockSpec(memory_space=pltpu.VMEM)
+    small = pl.BlockSpec(memory_space=pltpu.SMEM)
     return pl.pallas_call(
         kernel,
-        out_shape=(out, out, out),
-        in_specs=[held] * 8,
-        out_specs=(held, held, held),
-        scratch_shapes=[spec, spec, spec],
-        compiler_params=pltpu.CompilerParams(vmem_limit_bytes=48 * 1024 * 1024),
-    )(filter_wide, prod_wide, grad_wide, *tables(blocks, width))
-
-
-def exchange(value):
-    return lax.all_to_all(value, "ctx", split_axis=0, concat_axis=0, tiled=True)
+        out_shape=(moved, moved, moved, moved, line, line),
+        in_specs=[small] * 2 + [held] * 10,
+        out_specs=(held,) * 6,
+        scratch_shapes=[wide] * 8
+        + [spec] * 3
+        + [
+            pltpu.SemaphoreType.DMA((STREAMS,)),
+            pltpu.SemaphoreType.DMA((STREAMS,)),
+            pltpu.SemaphoreType.DMA((2,)),
+            pltpu.SemaphoreType.DMA((2,)),
+        ],
+        compiler_params=pltpu.CompilerParams(
+            collective_id=0, has_side_effects=True, vmem_limit_bytes=40 * 1024 * 1024
+        ),
+    )(docs, layers, handed, gate, key, inputs, filters, *tables(blocks, width))
 
 
 def body(handed_back, gate_q, key_k, input_x, filter_h, doc_lengths, section_layers):
     channels, width = gate_q.shape[2:]
     blocks = lax.axis_size("ctx")
-    pipe = lax.axis_size("pipe")
-    length = blocks * width
     shape = (blocks, channels // blocks, width)
-    layers = section_layers[lax.axis_index("pipe")]
-    scale = 1.0 / jnp.sqrt(layers.astype(jnp.float32))
-    spots = lax.axis_index("ctx") * width + jnp.arange(width, dtype=jnp.int32)
-    live = (spots < length - doc_lengths[0, -1]).astype(jnp.float32)
-    incoming = lax.ppermute(handed_back, "pipe", [(s, (s - 1) % pipe) for s in range(pipe)])
-    key32 = key_k.reshape(shape).astype(jnp.float32)
-    input32 = input_x.reshape(shape).astype(jnp.float32)
-    product = (key32 * input32 * live).astype(jnp.bfloat16)
-    first = exchange(jnp.stack([product, filter_h.reshape(shape)], axis=1))
-    grad32 = incoming.reshape(shape).astype(jnp.float32)
-    gate32 = gate_q.reshape(shape).astype(jnp.float32)
-    branch = exchange((scale * gate32 * grad32).astype(jnp.bfloat16))
-    results = spectra(first[:, 1], first[:, 0], branch)
-    home = exchange(jnp.stack(results, axis=1)).astype(jnp.float32)
-    conv32, corr32, lags = home[:, 0], home[:, 1], home[:, 2]
-    grad_gate = (scale * grad32 * conv32).astype(jnp.bfloat16)
+    blocked = [v.reshape(shape) for v in (handed_back, gate_q, key_k, input_x, filter_h)]
+    incoming, conv, corr, lags, live, scale = mixer(doc_lengths, section_layers, *blocked)
+    live, scale = live[0], scale[0]
+    key32 = blocked[2].astype(jnp.float32)
+    input32 = blocked[3].astype(jnp.float32)
+    grad32 = incoming.astype(jnp.float32)
+    corr32 = corr.astype(jnp.float32)
+    grad_gate = (scale * grad32 * conv.astype(jnp.float32)).astype(jnp.bfloat16)
     grad_key = (corr32 * input32 * live).astype(jnp.bfloat16)
     grad_input = (grad32 + corr32 * key32 * live).astype(jnp.bfloat16)
-    grad_filter = lags / math.sqrt(length)
+    grad_filter = lags.astype(jnp.float32) / math.sqrt(blocks * width)
     flat = gate_q.shape
     return (
         grad_input.reshape(flat),

time: 90.8 us -> 72.5 us (0.80)
  Pallas kernels: 3.92 us -> 59.7 us
  starting transfers between devices: 31.9 us -> 0 us
  waiting for transfers between devices: 27.3 us -> 0 us
  blocking collectives: 17.7 us -> 0 us
  local copies, waits for them, and re-layouts: 2.36 us -> 10.3 us
  other arithmetic: 4.95 us -> 1.35 us
  between operations: 2.19 us -> 0.68 us
    pallas_call x1, Pallas kernels: 3.92 us -> 59.7 us  [mixer(): pl.pallas_call(kernel, out_shape=(moved, moved, moved, moved, line, line)...]
    all_to_all x2 -> x0, starting transfers between devices: 21.3 us -> none  [exchange(): return lax.all_to_all(value, 'ctx', split_axis=0, concat_axis=0, tiled=True)]
    ppermute x1 -> x0, waiting for transfers between devices: 18.4 us -> none  [body(): lax.ppermute(handed_back, 'pipe', [(s, (s - 1) % pipe) for s in range(pip...]
    all_to_all x1 -> x0, blocking collectives: 17.7 us -> none  [exchange(): return lax.all_to_all(value, 'ctx', split_axis=0, concat_axis=0, tiled=True)]
    ppermute x1 -> x0, starting transfers between devices: 10.7 us -> none  [body(): lax.ppermute(handed_back, 'pipe', [(s, (s - 1) % pipe) for s in range(pip...]
    unnamed x22 -> x24, local copies, waits for them, and re-layouts: 0.28 us -> 10.3 us
    all_to_all x2 -> x0, waiting for transfers between devices: 8.92 us -> none  [exchange(): return lax.all_to_all(value, 'ctx', split_axis=0, concat_axis=0, tiled=True)]
    slice x2 -> x0, local copies, waits for them, and re-layouts: 1.4 us -> none  [the longest x1 1.28 us: body(): live = (spots < length - doc_lengths[0, -1]).astype(jnp.float32)]
  transfers between devices with their start and end apart: 3 -> 0, of which waited for: 2 -> 0; matrix products, arithmetic and copies ran while one was open for 2% -> 0% of each run, Pallas kernels for 0% -> 0%
where the time goes in v1:
time: 72.5 us; the launch traced here: 72 us
  Pallas kernels  59.7 us (82%)
  local copies, waits for them, and re-layouts  10.3 us (14%)
  other arithmetic  1.35 us (2%)
    pallas_call x1, Pallas kernels, mixer(): pl.pallas_call(kernel, out_shape=(moved, moved, moved, moved, line, line)...  59.7 us
    unnamed x24, local copies, waits for them, and re-layouts  10.3 us

profile of v1, /device:TPU:1, one launch (start us, length us, event | category | flops | bytes accessed | tf_op | source)
XLA Modules:
  0.0 72.0 jit_solution(12662360631625591258)
XLA Ops:
  0.6 0.0 copy-start.10
  0.6 0.0 copy-start.11
  0.7 0.6 copy-done.10
  1.3 0.0 copy-done.11
  1.3 0.0 copy-start
  1.3 0.9 %copy-done = bf16[1,1,1024,128]{3,2,1,0:T(8,128)(2,1)S(1)} copy-done((bf16[1,1,1024,128]{3,2,1,0:T(8,128)(2,1)S(1)}, bf16[1,1,1024,128]{3,2,1,0:T(8,128)(2,1)}, u32[]{:S(2)}) %copy-start) | copy-done | bytes 262168
  2.3 0.0 copy-start.1
  2.3 0.9 %copy-done.1 = bf16[1,1,1024,128]{3,2,1,0:T(8,128)(2,1)S(1)} copy-done((bf16[1,1,1024,128]{3,2,1,0:T(8,128)(2,1)S(1)}, bf16[1,1,1024,128]{3,2,1,0:T(8,128)(2,1)}, u32[]{:S(2)}) %copy-start.1) | copy-done | bytes 262168
  3.2 0.0 copy-start.2
  3.2 1.0 %copy-done.2 = bf16[2,256,512]{2,1,0:T(8,128)(2,1)S(1)} copy-done((bf16[2,256,512]{2,1,0:T(8,128)(2,1)S(1)}, bf16[2,256,512]{2,1,0:T(8,128)(2,1)}, u32[]{:S(2)}) %copy-start.2) | copy-done | bytes 524312
  4.2 0.0 copy-start.3
  4.3 1.0 %copy-done.3 = bf16[2,512,256]{2,1,0:T(8,128)(2,1)S(1)} copy-done((bf16[2,512,256]{2,1,0:T(8,128)(2,1)S(1)}, bf16[2,512,256]{2,1,0:T(8,128)(2,1)}, u32[]{:S(2)}) %copy-start.3) | copy-done | bytes 524312
  5.3 0.0 copy-start.4
  5.3 0.9 %copy-done.4 = bf16[1,1,1024,128]{3,2,1,0:T(8,128)(2,1)S(1)} copy-done((bf16[1,1,1024,128]{3,2,1,0:T(8,128)(2,1)S(1)}, bf16[1,1,1024,128]{3,2,1,0:T(8,128)(2,1)}, u32[]{:S(2)}) %copy-start.4) | copy-done | bytes 262168
  6.2 0.0 copy-start.5
  6.2 0.9 %copy-done.5 = bf16[1,1,1024,128]{3,2,1,0:T(8,128)(2,1)S(1)} copy-done((bf16[1,1,1024,128]{3,2,1,0:T(8,128)(2,1)S(1)}, bf16[1,1,1024,128]{3,2,1,0:T(8,128)(2,1)}, u32[]{:S(2)}) %copy-start.5) | copy-done | bytes 262168
  7.2 0.0 copy-start.6
  7.2 0.9 %copy-done.6 = bf16[1,1024,128]{2,1,0:T(8,128)(2,1)S(1)} copy-done((bf16[1,1024,128]{2,1,0:T(8,128)(2,1)S(1)}, bf16[1,1024,128]{2,1,0:T(8,128)(2,1)}, u32[]{:S(2)}) %copy-start.6) | copy-done | bytes 262168
  8.1 0.0 copy-start.7
  8.1 0.9 %copy-done.7 = f32[2,256,128]{2,1,0:T(8,128)S(1)} copy-done((f32[2,256,128]{2,1,0:T(8,128)S(1)}, f32[2,256,128]{2,1,0:T(8,128)}, u32[]{:S(2)}) %copy-start.7) | copy-done | bytes 262168
  9.1 0.0 copy-start.8
  9.1 0.9 %copy-done.8 = bf16[2,256,256]{2,1,0:T(8,128)(2,1)S(1)} copy-done((bf16[2,256,256]{2,1,0:T(8,128)(2,1)S(1)}, bf16[2,256,256]{2,1,0:T(8,128)(2,1)}, u32[]{:S(2)}) %copy-start.8) | copy-done | bytes 262168
  10.0 0.0 copy-start.9
  10.0 0.9 %copy-done.9 = bf16[2,256,256]{2,1,0:T(8,128)(2,1)S(1)} copy-done((bf16[2,256,256]{2,1,0:T(8,128)(2,1)S(1)}, bf16[2,256,256]{2,1,0:T(8,128)(2,1)}, u32[]{:S(2)}) %copy-start.9) | copy-done | bytes 262168
  11.0 59.7 %shard_map.147 = (bf16[32,32,128]{2,1,0:T(8,128)(2,1)S(1)}, bf16[32,32,128]{2,1,0:T(8,128)(2,1)S(1)}, bf16[32,32,128]{2,1,0:T(8,128)(2,1)S(1)}, bf16[32,32,128]{...) custom-call(s32[1,8]{1,0:T(1,128)S(1)} %copy-done.10, s32[4]{0:T(128)S(1)} %copy-done.11, ...), custom_call_target="tpu_custom_call" | custom-call | tf_op jit(solution)/shard_map/pallas_call | solution.py:238
  70.7 1.4 %fusion.5 = (bf16[32,32,128]{2,1,0:T(8,128)(2,1)}, bf16[32,32,128]{2,1,0:T(8,128)(2,1)}, bf16[32,32,128]{2,1,0:T(8,128)(2,1)}, f32[32,32,128]{2,1,0:T(8,128)}) fusion(bf16[32,32,128]{2,1,0:T(8,128)(2,1)S(1)} %get-tuple-element.11, bf16[32,32,128]{2,1,0:T(8,128)(2,1)S(1)} %bitcast.16, f32[128]{0:T(128)S(1)} %slice_bitcast_fusion.1, ...), kind=kLoop, calls=%fused_computation.9 | loop fusion | flops 2228224 | bytes 2884608 | tf_op jit(solution)/shard_map/convert_element_type | solution.py:269
  (2 shorter events, 0.0 us)
Async XLA Ops:
  0.6 0.7 copy-start.10
  0.6 0.7 copy-start.11
  1.3 0.9 %copy-start = (bf16[1,1,1024,128]{3,2,1,0:T(8,128)(2,1)S(1)}, bf16[1,1,1024,128]{3,2,1,0:T(8,128)(2,1)}, u32[]{:S(2)}) copy-start(bf16[1,1,1024,128]{3,2,1,0:T(8,128)(2,1)} %param.14) | copy-start | bytes 786436
  2.3 0.9 %copy-start.1 = (bf16[1,1,1024,128]{3,2,1,0:T(8,128)(2,1)S(1)}, bf16[1,1,1024,128]{3,2,1,0:T(8,128)(2,1)}, u32[]{:S(2)}) copy-start(bf16[1,1,1024,128]{3,2,1,0:T(8,128)(2,1)} %param.15) | copy-start | bytes 786436
  3.2 1.0 %copy-start.2 = (bf16[2,256,512]{2,1,0:T(8,128)(2,1)S(1)}, bf16[2,256,512]{2,1,0:T(8,128)(2,1)}, u32[]{:S(2)}) copy-start(bf16[2,256,512]{2,1,0:T(8,128)(2,1)} %constant.14.clone.gather_ref) | copy-start | bytes 1572868
  4.2 1.0 %copy-start.3 = (bf16[2,512,256]{2,1,0:T(8,128)(2,1)S(1)}, bf16[2,512,256]{2,1,0:T(8,128)(2,1)}, u32[]{:S(2)}) copy-start(bf16[2,512,256]{2,1,0:T(8,128)(2,1)} %constant.13.clone.spread_ref) | copy-start | bytes 1572868
  5.3 0.9 %copy-start.4 = (bf16[1,1,1024,128]{3,2,1,0:T(8,128)(2,1)S(1)}, bf16[1,1,1024,128]{3,2,1,0:T(8,128)(2,1)}, u32[]{:S(2)}) copy-start(bf16[1,1,1024,128]{3,2,1,0:T(8,128)(2,1)} %param.12) | copy-start | bytes 786436
  6.2 0.9 %copy-start.5 = (bf16[1,1,1024,128]{3,2,1,0:T(8,128)(2,1)S(1)}, bf16[1,1,1024,128]{3,2,1,0:T(8,128)(2,1)}, u32[]{:S(2)}) copy-start(bf16[1,1,1024,128]{3,2,1,0:T(8,128)(2,1)} %param.13) | copy-start | bytes 786436
  7.2 0.9 %copy-start.6 = (bf16[1,1024,128]{2,1,0:T(8,128)(2,1)S(1)}, bf16[1,1024,128]{2,1,0:T(8,128)(2,1)}, u32[]{:S(2)}) copy-start(bf16[1,1024,128]{2,1,0:T(8,128)(2,1)} %param.16) | copy-start | bytes 786436
  8.1 0.9 %copy-start.7 = (f32[2,256,128]{2,1,0:T(8,128)S(1)}, f32[2,256,128]{2,1,0:T(8,128)}, u32[]{:S(2)}) copy-start(f32[2,256,128]{2,1,0:T(8,128)} %constant.17.clone.turns_ref) | copy-start | bytes 786436
  9.1 0.9 %copy-start.8 = (bf16[2,256,256]{2,1,0:T(8,128)(2,1)S(1)}, bf16[2,256,256]{2,1,0:T(8,128)(2,1)}, u32[]{:S(2)}) copy-start(bf16[2,256,256]{2,1,0:T(8,128)(2,1)} %constant.16.clone.back_ref) | copy-start | bytes 786436
  10.0 0.9 %copy-start.9 = (bf16[2,256,256]{2,1,0:T(8,128)(2,1)S(1)}, bf16[2,256,256]{2,1,0:T(8,128)(2,1)}, u32[]{:S(2)}) copy-start(bf16[2,256,256]{2,1,0:T(8,128)(2,1)} %constant.15.clone.ahead_ref) | copy-start | bytes 786436

commit v2 on v1

--- a/solution.py
+++ b/solution.py
@@ -106,12 +106,13 @@
 
 
 def kernel(
-    docs_ref, layers_ref, handed_ref, gate_ref, key_ref, input_ref, filter_ref,
-    spread_ref, gather_ref, ahead_ref, back_ref, turns_ref,
+    docs_ref, layers_ref, handed_ref, gate_home, key_home, input_home, filter_ref,
+    spread_home, gather_home, ahead_home, back_home, turns_home,
     incoming_ref, conv_ref, corr_ref, lag_ref, live_ref, scale_ref,
     prod_out, grad_out, filter_wide, prod_wide, grad_wide, conv_wide, corr_wide, lag_wide,
     filter_spec, prod_spec, grad_spec,
-    send_sems, recv_sems, relay_send, relay_recv,
+    gate_ref, key_ref, input_ref, spread_ref, gather_ref, ahead_ref, back_ref, turns_ref,
+    send_sems, recv_sems, relay_send, relay_recv, load_sems,
 ):
     blocks, channels, width = key_ref.shape
     me = lax.axis_index("ctx")
@@ -148,7 +149,6 @@
             return carry
 
         lax.fori_loop(1, blocks, step, 0)
-        target[me, span, :] = source[me, span, :]
 
     def settle(buffer, span, stream):
         others = buffer.at[pl.ds(0, blocks - 1), span, :]
@@ -161,6 +161,25 @@
             device_id_type=MESH,
         )
 
+    def keep(source, target, span):
+        target[me, span, :] = source[me, span, :]
+
+    loads = [
+        pltpu.make_async_copy(source, target, load_sems.at[index])
+        for index, (source, target) in enumerate(
+            [
+                (key_home, key_ref),
+                (input_home, input_ref),
+                (spread_home, spread_ref),
+                (ahead_home, ahead_ref),
+                (turns_home, turns_ref),
+                (back_home, back_ref),
+                (gather_home, gather_ref),
+                (gate_home, gate_ref),
+                (filter_ref.at[me], filter_wide.at[me]),
+            ]
+        )
+    ]
     barrier = pltpu.get_barrier_semaphore()
 
     def greet(index, carry):
@@ -172,6 +191,8 @@
     for neighbour in (before, after):
         pl.semaphore_signal(barrier, inc=1, device_id={"pipe": neighbour}, device_id_type=MESH)
     lax.fori_loop(1, blocks, greet, 0)
+    for load in loads:
+        load.start()
 
     spots = me * width + lax.broadcasted_iota(jnp.int32, live_ref.shape, 1)
     limit = blocks * width - docs_ref[0, docs_ref.shape[1] - 1]
@@ -180,6 +201,8 @@
     scale_ref[...] = 1.0 / jnp.sqrt(layers.astype(jnp.float32))
     live = live_ref[:1, :][None]
     scale = scale_ref[:1, :][None]
+    loads[0].wait()
+    loads[1].wait()
     prod_out[...] = (
         key_ref[...].astype(jnp.float32) * input_ref[...].astype(jnp.float32) * live
     ).astype(jnp.bfloat16)
@@ -189,6 +212,9 @@
         relay(pair).start()
     scatter(filter_ref, filter_wide, whole, FILTER)
     scatter(prod_out, prod_wide, whole, PRODUCT)
+    keep(prod_out, prod_wide, whole)
+    for load in loads[2:]:
+        load.wait()
     settle(filter_wide, whole, FILTER).wait_recv()
     transform(filter_wide, filter_spec, range(pairs), spread_ref, ahead_ref, turns_ref)
     settle(prod_wide, whole, PRODUCT).wait_recv()
@@ -197,6 +223,7 @@
         filter_spec, prod_spec, False, conv_wide, range(pairs), gather_ref, back_ref, turns_ref
     )
     scatter(conv_wide, conv_ref, whole, CONV)
+    keep(conv_wide, conv_ref, whole)
 
     for pair in range(pairs):
         span = part(pair)
@@ -207,14 +234,17 @@
             * incoming_ref[:, span, :].astype(jnp.float32)
         ).astype(jnp.bfloat16)
         scatter(grad_out, grad_wide, span, GRAD + pair)
+        keep(grad_out, grad_wide, span)
         settle(grad_wide, span, GRAD + pair).wait_recv()
         transform(grad_wide, grad_spec, [pair], spread_ref, ahead_ref, turns_ref)
         multiply(
             filter_spec, grad_spec, True, corr_wide, [pair], gather_ref, back_ref, turns_ref
         )
         scatter(corr_wide, corr_ref, span, CORR + pair)
+        keep(corr_wide, corr_ref, span)
         multiply(prod_spec, grad_spec, True, lag_wide, [pair], gather_ref, back_ref, turns_ref)
         scatter(lag_wide, lag_ref, span, LAG + pair)
+        keep(lag_wide, lag_ref, span)
 
     settle(conv_ref, whole, CONV).wait_recv()
     settle(filter_wide, whole, FILTER).wait_send()
@@ -235,23 +265,28 @@
     spec = pltpu.VMEM((channels // GROUP, blocks * GROUP, 2 * width), jnp.float32)
     held = pl.BlockSpec(memory_space=pltpu.VMEM)
     small = pl.BlockSpec(memory_space=pltpu.SMEM)
+    far = pl.BlockSpec(memory_space=pl.ANY)
+    fixed = tables(blocks, width)
     return pl.pallas_call(
         kernel,
         out_shape=(moved, moved, moved, moved, line, line),
-        in_specs=[small] * 2 + [held] * 10,
+        in_specs=[small] * 2 + [far] * 10,
         out_specs=(held,) * 6,
         scratch_shapes=[wide] * 8
         + [spec] * 3
+        + [wide] * 3
+        + [pltpu.VMEM(table.shape, table.dtype) for table in fixed]
         + [
             pltpu.SemaphoreType.DMA((STREAMS,)),
             pltpu.SemaphoreType.DMA((STREAMS,)),
             pltpu.SemaphoreType.DMA((2,)),
             pltpu.SemaphoreType.DMA((2,)),
+            pltpu.SemaphoreType.DMA((9,)),
         ],
         compiler_params=pltpu.CompilerParams(
-            collective_id=0, has_side_effects=True, vmem_limit_bytes=40 * 1024 * 1024
+            collective_id=0, has_side_effects=True, vmem_limit_bytes=60 * 1024 * 1024
         ),
-    )(docs, layers, handed, gate, key, inputs, filters, *tables(blocks, width))
+    )(docs, layers, handed, gate, key, inputs, filters, *fixed)
 
 
 def body(handed_back, gate_q, key_k, input_x, filter_h, doc_lengths, section_layers):

time: 72.5 us -> 66 us (0.910)
  local copies, waits for them, and re-layouts: 10.3 us -> 1.37 us
  Pallas kernels: 59.7 us -> 61.2 us
  other arithmetic: 1.35 us -> 2.54 us
    unnamed x24 -> x4, local copies, waits for them, and re-layouts: 10.3 us -> 0.01 us
    pallas_call x1, Pallas kernels: 59.7 us -> 61.2 us  [mixer(): pl.pallas_call(kernel, out_shape=(moved, moved, moved, moved, line, line)...]
    convert_element_type x1, other arithmetic: 1.35 us -> 2.54 us  [body(): grad_key = (corr32 * input32 * live).astype(jnp.bfloat16)]
where the time goes in v2:
time: 66 us; the launch traced here: 65.8 us
  Pallas kernels  61.2 us (93%)
  other arithmetic  2.54 us (4%)
  local copies, waits for them, and re-layouts  1.37 us (2%)
  between operations  0.66 us (1%)
    pallas_call x1, Pallas kernels, mixer(): pl.pallas_call(kernel, out_shape=(moved, moved, moved, moved, line, line)...  61.2 us
    convert_element_type x1, other arithmetic, body(): grad_key = (corr32 * input32 * live).astype(jnp.bfloat16)  2.54 us

profile of v2, /device:TPU:1, one launch (start us, length us, event | category | flops | bytes accessed | tf_op | source)
XLA Modules:
  0.0 65.8 jit_solution(12957562735953700963)
XLA Ops:
  0.6 0.0 copy-start
  0.6 0.0 copy-start.1
  0.7 61.2 %shard_map.147 = (bf16[32,32,128]{2,1,0:T(8,128)(2,1)}, bf16[32,32,128]{2,1,0:T(8,128)(2,1)}, bf16[32,32,128]{2,1,0:T(8,128)(2,1)}, bf16[32,32,128]{2,1,0:T(8,12...) custom-call(s32[1,8]{1,0:T(1,128)} %docs_ref.1, s32[4]{0:T(128)} %layers_ref.1, bf16[32,32,128]{2,1,0:T(8,128)(2,1)} %bitcast.18, ...), custom_call_target="tpu_custom_call" | custom-call | tf_op jit(solution)/shard_map/pallas_call | solution.py:270
  61.9 0.7 %slice_bitcast_fusion.1 = f32[128]{0:T(128)S(1)} fusion(f32[8,128]{1,0:T(8,128)} %get-tuple-element.12), kind=kLoop, calls=%fused_computation.12 | loop fusion | bytes 1024 | tf_op jit(solution)/shard_map/mul | solution.py:305
  62.6 0.7 %slice_bitcast_fusion = f32[128]{0:T(128)S(1)} fusion(f32[8,128]{1,0:T(8,128)} %get-tuple-element.13), kind=kLoop, calls=%fused_computation.11 | loop fusion | bytes 1024 | tf_op jit(solution)/shard_map/mul | solution.py:303
  63.2 0.0 copy-done
  63.2 0.0 copy-done.1
  63.2 2.5 %fusion.5 = (bf16[32,32,128]{2,1,0:T(8,128)(2,1)}, bf16[32,32,128]{2,1,0:T(8,128)(2,1)}, bf16[32,32,128]{2,1,0:T(8,128)(2,1)}, f32[32,32,128]{2,1,0:T(8,128)}) fusion(bf16[32,32,128]{2,1,0:T(8,128)(2,1)} %get-tuple-element.11, bf16[32,32,128]{2,1,0:T(8,128)(2,1)S(1)} %bitcast.16, f32[128]{0:T(128)S(1)} %slice_bitcast_fusion.1, ...), kind=kLoop, calls=%fused_computation.9 | loop fusion | flops 2228224 | bytes 2884608 | tf_op jit(solution)/shard_map/convert_element_type | solution.py:304
Async XLA Ops:
  0.6 62.6 %copy-start = (bf16[1,1,1024,128]{3,2,1,0:T(8,128)(2,1)S(1)}, bf16[1,1,1024,128]{3,2,1,0:T(8,128)(2,1)}, u32[]{:S(2)}) copy-start(bf16[1,1,1024,128]{3,2,1,0:T(8,128)(2,1)} %param.14) | copy-start | bytes 786436
  0.6 62.6 %copy-start.1 = (bf16[1,1,1024,128]{3,2,1,0:T(8,128)(2,1)S(1)}, bf16[1,1,1024,128]{3,2,1,0:T(8,128)(2,1)}, u32[]{:S(2)}) copy-start(bf16[1,1,1024,128]{3,2,1,0:T(8,128)(2,1)} %param.15) | copy-start | bytes 786436

commit v3 on v2

--- a/solution.py
+++ b/solution.py
@@ -49,14 +49,19 @@
     )
 
 
-def transform(wide_ref, spec_ref, pairs, spread_ref, ahead_ref, turns_ref):
+def transform(wide_ref, spec_ref, span, spread_ref, ahead_ref, turns_ref):
     blocks, channels, width = wide_ref.shape
     rows = blocks * GROUP
-    for pair in pairs:
-        chunk = wide_ref[:, 2 * GROUP * pair : 2 * GROUP * (pair + 1), :].astype(jnp.float32)
-        sides = [chunk[:, :GROUP, :].reshape(rows, width), chunk[:, GROUP:, :].reshape(rows, width)]
+    first, count = span
+    for start in range(first, first + count, 2):
+        groups = range(start, min(start + 2, first + count))
+        chunk = wide_ref[:, GROUP * start : GROUP * (groups[-1] + 1), :].astype(jnp.float32)
+        sides = [
+            chunk[:, GROUP * (g - start) : GROUP * (g - start + 1), :].reshape(rows, width)
+            for g in groups
+        ]
         mixed = fixed_left(spread_ref, jnp.concatenate(sides, axis=1).astype(jnp.bfloat16))
-        for side in range(2):
+        for side, group in enumerate(groups):
             part = mixed[:, side * width : (side + 1) * width]
             part_re, part_im = part[:rows], part[rows:]
             turned = jnp.concatenate(
@@ -66,16 +71,17 @@
                 ],
                 axis=1,
             )
-            spec_ref[2 * pair + side] = fixed_right(turned.astype(jnp.bfloat16), ahead_ref)
-
-
-def multiply(left_ref, right_ref, conjugate, wide_ref, pairs, gather_ref, back_ref, turns_ref):
+            spec_ref[group] = fixed_right(turned.astype(jnp.bfloat16), ahead_ref)
+
+
+def multiply(left_ref, right_ref, conjugate, wide_ref, span, gather_ref, back_ref, turns_ref):
     blocks, channels, width = wide_ref.shape
-    rows = blocks * GROUP
-    for pair in pairs:
+    first, count = span
+    for start in range(first, first + count, 2):
+        groups = range(start, min(start + 2, first + count))
         sides = []
-        for side in range(2):
-            left, right = left_ref[2 * pair + side], right_ref[2 * pair + side]
+        for group in groups:
+            left, right = left_ref[group], right_ref[group]
             left_re, left_im = left[:, :width], left[:, width:]
             right_re, right_im = right[:, :width], right[:, width:]
             if conjugate:
@@ -96,13 +102,17 @@
                 )
             )
         signal = fixed_left(gather_ref, jnp.concatenate(sides, axis=1).astype(jnp.bfloat16))
-        outs = [signal[:, s * width : (s + 1) * width].reshape(blocks, GROUP, width) for s in range(2)]
+        outs = [
+            signal[:, s * width : (s + 1) * width].reshape(blocks, GROUP, width)
+            for s in range(len(sides))
+        ]
         chunk = jnp.concatenate(outs, axis=1).astype(jnp.bfloat16)
-        wide_ref[:, 2 * GROUP * pair : 2 * GROUP * (pair + 1), :] = chunk
+        wide_ref[:, GROUP * start : GROUP * (groups[-1] + 1), :] = chunk
+
 
 MESH = pl.DeviceIdType.MESH
-FILTER, PRODUCT, CONV, GRAD, CORR, LAG = 0, 1, 2, 3, 5, 7
-STREAMS = 9
+FILTER, PRODUCT, CONV, GRAD, CORR, LAG = 0, 1, 2, 3, 6, 9
+STREAMS = 12
 
 
 def kernel(
@@ -119,18 +129,21 @@
     section, sections = lax.axis_index("pipe"), lax.axis_size("pipe")
     before = lax.rem(section + sections - 1, sections)
     after = lax.rem(section + 1, sections)
-    pairs = channels // (2 * GROUP)
-    whole = pl.ds(0, channels)
-
-    def part(pair):
-        return pl.ds(2 * GROUP * pair, 2 * GROUP)
-
-    def relay(pair):
+    groups = channels // GROUP
+    whole, every = pl.ds(0, channels), (0, groups)
+    quarter = groups // 4
+    pieces = [(0, groups - 2 * quarter), (groups - 2 * quarter, quarter), (groups - quarter, quarter)]
+
+    def part(piece):
+        first, count = pieces[piece]
+        return pl.ds(GROUP * first, GROUP * count)
+
+    def relay(piece):
         return pltpu.make_async_remote_copy(
-            src_ref=handed_ref.at[:, part(pair), :],
-            dst_ref=incoming_ref.at[:, part(pair), :],
-            send_sem=relay_send.at[pair],
-            recv_sem=relay_recv.at[pair],
+            src_ref=handed_ref.at[:, part(piece), :],
+            dst_ref=incoming_ref.at[:, part(piece), :],
+            send_sem=relay_send.at[piece],
+            recv_sem=relay_recv.at[piece],
             device_id={"pipe": before},
             device_id_type=MESH,
         )
@@ -199,8 +212,8 @@
     live_ref[...] = (spots < limit).astype(jnp.float32)
     layers = jnp.full(scale_ref.shape, layers_ref[section], jnp.int32)
     scale_ref[...] = 1.0 / jnp.sqrt(layers.astype(jnp.float32))
-    live = live_ref[:1, :][None]
-    scale = scale_ref[:1, :][None]
+    live = live_ref[...][None]
+    scale = scale_ref[...][None]
     loads[0].wait()
     loads[1].wait()
     prod_out[...] = (
@@ -208,59 +221,59 @@
     ).astype(jnp.bfloat16)
     pl.semaphore_wait(barrier, blocks + 1)
 
-    for pair in range(pairs):
-        relay(pair).start()
+    for piece in range(len(pieces)):
+        relay(piece).start()
     scatter(filter_ref, filter_wide, whole, FILTER)
     scatter(prod_out, prod_wide, whole, PRODUCT)
     keep(prod_out, prod_wide, whole)
     for load in loads[2:]:
         load.wait()
     settle(filter_wide, whole, FILTER).wait_recv()
-    transform(filter_wide, filter_spec, range(pairs), spread_ref, ahead_ref, turns_ref)
+    transform(filter_wide, filter_spec, every, spread_ref, ahead_ref, turns_ref)
     settle(prod_wide, whole, PRODUCT).wait_recv()
-    transform(prod_wide, prod_spec, range(pairs), spread_ref, ahead_ref, turns_ref)
+    transform(prod_wide, prod_spec, every, spread_ref, ahead_ref, turns_ref)
     multiply(
-        filter_spec, prod_spec, False, conv_wide, range(pairs), gather_ref, back_ref, turns_ref
+        filter_spec, prod_spec, False, conv_wide, every, gather_ref, back_ref, turns_ref
     )
     scatter(conv_wide, conv_ref, whole, CONV)
     keep(conv_wide, conv_ref, whole)
 
-    for pair in range(pairs):
-        span = part(pair)
-        relay(pair).wait_recv()
+    for piece in range(len(pieces)):
+        span = part(piece)
+        relay(piece).wait_recv()
         grad_out[:, span, :] = (
             scale
             * gate_ref[:, span, :].astype(jnp.float32)
             * incoming_ref[:, span, :].astype(jnp.float32)
         ).astype(jnp.bfloat16)
-        scatter(grad_out, grad_wide, span, GRAD + pair)
+        scatter(grad_out, grad_wide, span, GRAD + piece)
         keep(grad_out, grad_wide, span)
-        settle(grad_wide, span, GRAD + pair).wait_recv()
-        transform(grad_wide, grad_spec, [pair], spread_ref, ahead_ref, turns_ref)
+        settle(grad_wide, span, GRAD + piece).wait_recv()
+        transform(grad_wide, grad_spec, pieces[piece], spread_ref, ahead_ref, turns_ref)
         multiply(
-            filter_spec, grad_spec, True, corr_wide, [pair], gather_ref, back_ref, turns_ref
-        )
-        scatter(corr_wide, corr_ref, span, CORR + pair)
+            filter_spec, grad_spec, True, corr_wide, pieces[piece], gather_ref, back_ref, turns_ref
+        )
+        scatter(corr_wide, corr_ref, span, CORR + piece)
         keep(corr_wide, corr_ref, span)
-        multiply(prod_spec, grad_spec, True, lag_wide, [pair], gather_ref, back_ref, turns_ref)
-        scatter(lag_wide, lag_ref, span, LAG + pair)
+        multiply(prod_spec, grad_spec, True, lag_wide, pieces[piece], gather_ref, back_ref, turns_ref)
+        scatter(lag_wide, lag_ref, span, LAG + piece)
         keep(lag_wide, lag_ref, span)
 
     settle(conv_ref, whole, CONV).wait_recv()
     settle(filter_wide, whole, FILTER).wait_send()
     settle(prod_wide, whole, PRODUCT).wait_send()
     settle(conv_ref, whole, CONV).wait_send()
-    for pair in range(pairs):
-        relay(pair).wait_send()
-        settle(grad_wide, part(pair), GRAD + pair).wait_send()
-        settle(corr_ref, part(pair), CORR + pair).wait()
-        settle(lag_ref, part(pair), LAG + pair).wait()
+    for piece in range(len(pieces)):
+        relay(piece).wait_send()
+        settle(grad_wide, part(piece), GRAD + piece).wait_send()
+        settle(corr_ref, part(piece), CORR + piece).wait()
+        settle(lag_ref, part(piece), LAG + piece).wait()
 
 
 def mixer(docs, layers, handed, gate, key, inputs, filters):
     blocks, channels, width = key.shape
     moved = jax.ShapeDtypeStruct(key.shape, jnp.bfloat16)
-    line = jax.ShapeDtypeStruct((8, width), jnp.float32)
+    line = jax.ShapeDtypeStruct((1, width), jnp.float32)
     wide = pltpu.VMEM(key.shape, jnp.bfloat16)
     spec = pltpu.VMEM((channels // GROUP, blocks * GROUP, 2 * width), jnp.float32)
     held = pl.BlockSpec(memory_space=pltpu.VMEM)
@@ -279,8 +292,8 @@
         + [
             pltpu.SemaphoreType.DMA((STREAMS,)),
             pltpu.SemaphoreType.DMA((STREAMS,)),
-            pltpu.SemaphoreType.DMA((2,)),
-            pltpu.SemaphoreType.DMA((2,)),
+            pltpu.SemaphoreType.DMA((3,)),
+            pltpu.SemaphoreType.DMA((3,)),
             pltpu.SemaphoreType.DMA((9,)),
         ],
         compiler_params=pltpu.CompilerParams(
@@ -295,7 +308,7 @@
     shape = (blocks, channels // blocks, width)
     blocked = [v.reshape(shape) for v in (handed_back, gate_q, key_k, input_x, filter_h)]
     incoming, conv, corr, lags, live, scale = mixer(doc_lengths, section_layers, *blocked)
-    live, scale = live[0], scale[0]
+    live, scale = live[None], scale[None]
     key32 = blocked[2].astype(jnp.float32)
     input32 = blocked[3].astype(jnp.float32)
     grad32 = incoming.astype(jnp.float32)

time: 66 us -> 72.3 us (1.095)
  Pallas kernels: 61.2 us -> 68.2 us
  local copies, waits for them, and re-layouts: 1.37 us -> 0.64 us
    pallas_call x1, Pallas kernels: 61.2 us -> 68.2 us  [mixer(): pl.pallas_call(kernel, out_shape=(moved, moved, moved, moved, line, line)...]
    mul x2 -> x0, local copies, waits for them, and re-layouts: 1.36 us -> none  [the longest x1 0.69 us: body(): grad_gate = (scale * grad32 * conv.astype(jnp.float32)).astype(jnp.bfloat16)]
where the time goes in v3:
time: 72.3 us; the launch traced here: 72.1 us
  Pallas kernels  68.2 us (94%)
  other arithmetic  2.54 us (4%)
    pallas_call x1, Pallas kernels, mixer(): pl.pallas_call(kernel, out_shape=(moved, moved, moved, moved, line, line)...  68.2 us
    convert_element_type x1, other arithmetic, body(): grad_key = (corr32 * input32 * live).astype(jnp.bfloat16)  2.54 us

profile of v3, /device:TPU:1, one launch (start us, length us, event | category | flops | bytes accessed | tf_op | source)
XLA Modules:
  0.0 72.1 jit_solution(8234556304565375043)
XLA Ops:
  0.6 0.0 copy-start
  0.6 0.0 copy-start.1
  0.7 68.2 %shard_map.147 = (bf16[32,32,128]{2,1,0:T(8,128)(2,1)}, bf16[32,32,128]{2,1,0:T(8,128)(2,1)}, bf16[32,32,128]{2,1,0:T(8,128)(2,1)}, bf16[32,32,128]{2,1,0:T(8,12...) custom-call(s32[1,8]{1,0:T(1,128)} %docs_ref.1, s32[4]{0:T(128)} %layers_ref.1, bf16[32,32,128]{2,1,0:T(8,128)(2,1)} %bitcast.16, ...), custom_call_target="tpu_custom_call" | custom-call | tf_op jit(solution)/shard_map/pallas_call | solution.py:283
  68.9 0.0 copy-start.2
  68.9 0.0 copy-start.3
  68.9 0.0 copy-done
  68.9 0.0 copy-done.1
  68.9 0.6 copy-done.2
  69.5 0.0 copy-done.3
  69.6 2.5 %fusion.5 = (bf16[32,32,128]{2,1,0:T(8,128)(2,1)}, bf16[32,32,128]{2,1,0:T(8,128)(2,1)}, bf16[32,32,128]{2,1,0:T(8,128)(2,1)}, f32[32,32,128]{2,1,0:T(8,128)}) fusion(bf16[32,32,128]{2,1,0:T(8,128)(2,1)} %get-tuple-element.11, bf16[32,32,128]{2,1,0:T(8,128)(2,1)S(1)} %bitcast.14, f32[128]{0:T(128)S(1)} %bitcast.22, bf16[32,32,128]{2,1,0:T(8,128)(2,1)S(1)} %bitcast.12, ...), kind=kLoop, calls=%fused_computation.9 | loop fusion | flops 2228224 | bytes 2884608 | tf_op jit(solution)/shard_map/convert_element_type | solution.py:317
Async XLA Ops:
  0.6 68.3 %copy-start = (bf16[1,1,1024,128]{3,2,1,0:T(8,128)(2,1)S(1)}, bf16[1,1,1024,128]{3,2,1,0:T(8,128)(2,1)}, u32[]{:S(2)}) copy-start(bf16[1,1,1024,128]{3,2,1,0:T(8,128)(2,1)} %param.14) | copy-start | bytes 786436
  0.6 68.3 %copy-start.1 = (bf16[1,1,1024,128]{3,2,1,0:T(8,128)(2,1)S(1)}, bf16[1,1,1024,128]{3,2,1,0:T(8,128)(2,1)}, u32[]{:S(2)}) copy-start(bf16[1,1,1024,128]{3,2,1,0:T(8,128)(2,1)} %param.15) | copy-start | bytes 786436
  68.9 0.7 copy-start.2
  68.9 0.7 copy-start.3

commit v4 on v3

--- a/solution.py
+++ b/solution.py
@@ -107,19 +107,21 @@
             for s in range(len(sides))
         ]
         chunk = jnp.concatenate(outs, axis=1).astype(jnp.bfloat16)
-        wide_ref[:, GROUP * start : GROUP * (groups[-1] + 1), :] = chunk
+        wide_ref[:, GROUP * (start - first) : GROUP * (groups[-1] + 1 - first), :] = chunk
 
 
 MESH = pl.DeviceIdType.MESH
-FILTER, PRODUCT, CONV, GRAD, CORR, LAG = 0, 1, 2, 3, 6, 9
-STREAMS = 12
+PIECES = 2
+OUTWARD, CONV, GRAD, BACK = 0, 1, 2, 2 + PIECES
+STREAMS = 2 + 2 * PIECES
+LOADS = 9
 
 
 def kernel(
     docs_ref, layers_ref, handed_ref, gate_home, key_home, input_home, filter_ref,
     spread_home, gather_home, ahead_home, back_home, turns_home,
-    incoming_ref, conv_ref, corr_ref, lag_ref, live_ref, scale_ref,
-    prod_out, grad_out, filter_wide, prod_wide, grad_wide, conv_wide, corr_wide, lag_wide,
+    incoming_ref, conv_ref, both_ref, live_ref, scale_ref,
+    first_out, first_wide, grad_out, grad_wide, conv_wide, both_wide,
     filter_spec, prod_spec, grad_spec,
     gate_ref, key_ref, input_ref, spread_ref, gather_ref, ahead_ref, back_ref, turns_ref,
     send_sems, recv_sems, relay_send, relay_recv, load_sems,
@@ -129,31 +131,31 @@
     section, sections = lax.axis_index("pipe"), lax.axis_size("pipe")
     before = lax.rem(section + sections - 1, sections)
     after = lax.rem(section + 1, sections)
-    groups = channels // GROUP
-    whole, every = pl.ds(0, channels), (0, groups)
-    quarter = groups // 4
-    pieces = [(0, groups - 2 * quarter), (groups - 2 * quarter, quarter), (groups - quarter, quarter)]
-
-    def part(piece):
-        first, count = pieces[piece]
-        return pl.ds(GROUP * first, GROUP * count)
+    share = channels // PIECES
+    every = (0, channels // GROUP)
+
+    def part(ref, piece):
+        return ref.at[:, pl.ds(share * piece, share), :]
+
+    def groups(piece):
+        return (share * piece // GROUP, share // GROUP)
 
     def relay(piece):
         return pltpu.make_async_remote_copy(
-            src_ref=handed_ref.at[:, part(piece), :],
-            dst_ref=incoming_ref.at[:, part(piece), :],
+            src_ref=part(handed_ref, piece),
+            dst_ref=part(incoming_ref, piece),
             send_sem=relay_send.at[piece],
             recv_sem=relay_recv.at[piece],
             device_id={"pipe": before},
             device_id_type=MESH,
         )
 
-    def scatter(source, target, span, stream):
+    def scatter(source, target, stream):
         def step(index, carry):
             peer = lax.rem(me + index, blocks)
             pltpu.make_async_remote_copy(
-                src_ref=source.at[peer, span, :],
-                dst_ref=target.at[me, span, :],
+                src_ref=source.at[peer],
+                dst_ref=target.at[me],
                 send_sem=send_sems.at[stream],
                 recv_sem=recv_sems.at[stream],
                 device_id={"ctx": peer},
@@ -162,9 +164,10 @@
             return carry
 
         lax.fori_loop(1, blocks, step, 0)
-
-    def settle(buffer, span, stream):
-        others = buffer.at[pl.ds(0, blocks - 1), span, :]
+        target[me] = source[me]
+
+    def settle(buffer, stream):
+        others = buffer.at[pl.ds(0, blocks - 1)]
         return pltpu.make_async_remote_copy(
             src_ref=others,
             dst_ref=others,
@@ -174,22 +177,19 @@
             device_id_type=MESH,
         )
 
-    def keep(source, target, span):
-        target[me, span, :] = source[me, span, :]
-
     loads = [
         pltpu.make_async_copy(source, target, load_sems.at[index])
         for index, (source, target) in enumerate(
             [
                 (key_home, key_ref),
                 (input_home, input_ref),
+                (filter_ref, first_out.at[:, 0]),
                 (spread_home, spread_ref),
                 (ahead_home, ahead_ref),
                 (turns_home, turns_ref),
                 (back_home, back_ref),
                 (gather_home, gather_ref),
                 (gate_home, gate_ref),
-                (filter_ref.at[me], filter_wide.at[me]),
             ]
         )
     ]
@@ -214,67 +214,65 @@
     scale_ref[...] = 1.0 / jnp.sqrt(layers.astype(jnp.float32))
     live = live_ref[...][None]
     scale = scale_ref[...][None]
-    loads[0].wait()
-    loads[1].wait()
-    prod_out[...] = (
+    for load in loads[:3]:
+        load.wait()
+    first_out[:, 1] = (
         key_ref[...].astype(jnp.float32) * input_ref[...].astype(jnp.float32) * live
     ).astype(jnp.bfloat16)
     pl.semaphore_wait(barrier, blocks + 1)
 
-    for piece in range(len(pieces)):
+    for piece in range(PIECES):
         relay(piece).start()
-    scatter(filter_ref, filter_wide, whole, FILTER)
-    scatter(prod_out, prod_wide, whole, PRODUCT)
-    keep(prod_out, prod_wide, whole)
-    for load in loads[2:]:
+    scatter(first_out, first_wide, OUTWARD)
+    for load in loads[3:]:
         load.wait()
-    settle(filter_wide, whole, FILTER).wait_recv()
-    transform(filter_wide, filter_spec, every, spread_ref, ahead_ref, turns_ref)
-    settle(prod_wide, whole, PRODUCT).wait_recv()
-    transform(prod_wide, prod_spec, every, spread_ref, ahead_ref, turns_ref)
-    multiply(
-        filter_spec, prod_spec, False, conv_wide, every, gather_ref, back_ref, turns_ref
-    )
-    scatter(conv_wide, conv_ref, whole, CONV)
-    keep(conv_wide, conv_ref, whole)
-
-    for piece in range(len(pieces)):
-        span = part(piece)
+    settle(first_wide, OUTWARD).wait_recv()
+    transform(first_wide.at[:, 0], filter_spec, every, spread_ref, ahead_ref, turns_ref)
+    transform(first_wide.at[:, 1], prod_spec, every, spread_ref, ahead_ref, turns_ref)
+    multiply(filter_spec, prod_spec, False, conv_wide, every, gather_ref, back_ref, turns_ref)
+    scatter(conv_wide, conv_ref, CONV)
+
+    def send_grad(piece):
         relay(piece).wait_recv()
+        span = pl.ds(share * piece, share)
         grad_out[:, span, :] = (
             scale
             * gate_ref[:, span, :].astype(jnp.float32)
             * incoming_ref[:, span, :].astype(jnp.float32)
         ).astype(jnp.bfloat16)
-        scatter(grad_out, grad_wide, span, GRAD + piece)
-        keep(grad_out, grad_wide, span)
-        settle(grad_wide, span, GRAD + piece).wait_recv()
-        transform(grad_wide, grad_spec, pieces[piece], spread_ref, ahead_ref, turns_ref)
-        multiply(
-            filter_spec, grad_spec, True, corr_wide, pieces[piece], gather_ref, back_ref, turns_ref
-        )
-        scatter(corr_wide, corr_ref, span, CORR + piece)
-        keep(corr_wide, corr_ref, span)
-        multiply(prod_spec, grad_spec, True, lag_wide, pieces[piece], gather_ref, back_ref, turns_ref)
-        scatter(lag_wide, lag_ref, span, LAG + piece)
-        keep(lag_wide, lag_ref, span)
-
-    settle(conv_ref, whole, CONV).wait_recv()
-    settle(filter_wide, whole, FILTER).wait_send()
-    settle(prod_wide, whole, PRODUCT).wait_send()
-    settle(conv_ref, whole, CONV).wait_send()
-    for piece in range(len(pieces)):
+        scatter(part(grad_out, piece), part(grad_wide, piece), GRAD + piece)
+
+    def send_back(piece):
+        span = groups(piece)
+        settle(part(grad_wide, piece), GRAD + piece).wait_recv()
+        transform(grad_wide, grad_spec, span, spread_ref, ahead_ref, turns_ref)
+        for index, spec in enumerate((filter_spec, prod_spec)):
+            multiply(
+                spec, grad_spec, True, both_wide.at[:, piece, index], span,
+                gather_ref, back_ref, turns_ref,
+            )
+        scatter(both_wide.at[:, piece], both_ref.at[:, piece], BACK + piece)
+
+    for piece in range(PIECES):
+        send_grad(piece)
+    for piece in range(PIECES):
+        send_back(piece)
+
+    settle(conv_ref, CONV).wait()
+    settle(first_wide, OUTWARD).wait_send()
+    for piece in range(PIECES):
         relay(piece).wait_send()
-        settle(grad_wide, part(piece), GRAD + piece).wait_send()
-        settle(corr_ref, part(piece), CORR + piece).wait()
-        settle(lag_ref, part(piece), LAG + piece).wait()
+        settle(part(grad_wide, piece), GRAD + piece).wait_send()
+        settle(both_ref.at[:, piece], BACK + piece).wait()
 
 
 def mixer(docs, layers, handed, gate, key, inputs, filters):
     blocks, channels, width = key.shape
     moved = jax.ShapeDtypeStruct(key.shape, jnp.bfloat16)
+    both = (blocks, PIECES, 2, channels // PIECES, width)
     line = jax.ShapeDtypeStruct((1, width), jnp.float32)
     wide = pltpu.VMEM(key.shape, jnp.bfloat16)
+    double = pltpu.VMEM((blocks, 2, channels, width), jnp.bfloat16)
     spec = pltpu.VMEM((channels // GROUP, blocks * GROUP, 2 * width), jnp.float32)
     held = pl.BlockSpec(memory_space=pltpu.VMEM)
     small = pl.BlockSpec(memory_space=pltpu.SMEM)
@@ -282,19 +280,19 @@
     fixed = tables(blocks, width)
     return pl.pallas_call(
         kernel,
-        out_shape=(moved, moved, moved, moved, line, line),
+        out_shape=(moved, moved, jax.ShapeDtypeStruct(both, jnp.bfloat16), line, line),
         in_specs=[small] * 2 + [far] * 10,
-        out_specs=(held,) * 6,
-        scratch_shapes=[wide] * 8
+        out_specs=(held,) * 5,
+        scratch_shapes=[double, double, wide, wide, wide, pltpu.VMEM(both, jnp.bfloat16)]
         + [spec] * 3
         + [wide] * 3
         + [pltpu.VMEM(table.shape, table.dtype) for table in fixed]
         + [
             pltpu.SemaphoreType.DMA((STREAMS,)),
             pltpu.SemaphoreType.DMA((STREAMS,)),
-            pltpu.SemaphoreType.DMA((3,)),
-            pltpu.SemaphoreType.DMA((3,)),
-            pltpu.SemaphoreType.DMA((9,)),
+            pltpu.SemaphoreType.DMA((PIECES,)),
+            pltpu.SemaphoreType.DMA((PIECES,)),
+            pltpu.SemaphoreType.DMA((LOADS,)),
         ],
         compiler_params=pltpu.CompilerParams(
             collective_id=0, has_side_effects=True, vmem_limit_bytes=60 * 1024 * 1024
@@ -307,7 +305,8 @@
     blocks = lax.axis_size("ctx")
     shape = (blocks, channels // blocks, width)
     blocked = [v.reshape(shape) for v in (handed_back, gate_q, key_k, input_x, filter_h)]
-    incoming, conv, corr, lags, live, scale = mixer(doc_lengths, section_layers, *blocked)
+    incoming, conv, both, live, scale = mixer(doc_lengths, section_layers, *blocked)
+    corr, lags = [both[:, :, i].reshape(shape) for i in range(2)]
     live, scale = live[None], scale[None]
     key32 = blocked[2].astype(jnp.float32)
     input32 = blocked[3].astype(jnp.float32)

time: 72.3 us -> 60.6 us (0.84)
  Pallas kernels: 68.2 us -> 55.7 us
  other arithmetic: 2.54 us -> 3.67 us
    pallas_call x1, Pallas kernels: 68.2 us -> 55.7 us  [mixer(): pl.pallas_call(kernel, out_shape=(moved, moved, jax.ShapeDtypeStruct(both...]
    convert_element_type x0 -> x2, other arithmetic: none -> 2.03 us  [the longest x1 1.07 us: body(): corr32 = corr.astype(jnp.float32)]
    convert_element_type x1, other arithmetic: 2.54 us -> 0.78 us  [body(): grad_key = (corr32 * input32 * live).astype(jnp.bfloat16)]
    div x0 -> x1, other arithmetic: none -> 0.86 us  [body(): grad_filter = lags.astype(jnp.float32) / math.sqrt(blocks * width)]
where the time goes in v4:
time: 60.6 us; the launch traced here: 60.3 us
  Pallas kernels  55.7 us (92%)
  other arithmetic  3.67 us (6%)
  between operations  0.72 us (1%)
    pallas_call x1, Pallas kernels, mixer(): pl.pallas_call(kernel, out_shape=(moved, moved, jax.ShapeDtypeStruct(both...  55.7 us

profile of v4, /device:TPU:1, one launch (start us, length us, event | category | flops | bytes accessed | tf_op | source)
XLA Modules:
  0.0 60.3 jit_solution(11811303438350870860)
XLA Ops:
  0.6 55.7 %shard_map.147 = (bf16[32,32,128]{2,1,0:T(8,128)(2,1)}, bf16[32,32,128]{2,1,0:T(8,128)(2,1)}, bf16[32,2,2,16,128]{4,3,2,1,0:T(8,128)(2,1)}, f32[1,128]{1,0:T(1,128)}, f32[1,128]{1,0:T(1,128)}) custom-call(s32[1,8]{1,0:T(1,128)} %docs_ref.1, s32[4]{0:T(128)} %layers_ref.1, bf16[32,32,128]{2,1,0:T(8,128)(2,1)} %bitcast.22, bf16[32,32,128]{2,1,0:T(8,128)(2,1)} %bitcast.23, ...), custom_call_target="tpu_custom_call" | custom-call | tf_op jit(solution)/shard_map/pallas_call | solution.py:281
  56.3 0.0 copy-start.5
  56.3 0.0 copy-start.6
  56.3 0.0 copy-start
  56.4 0.0 copy-start.3
  56.4 0.0 copy-start.4
  56.4 1.1 %slice_convert_fusion = f32[32,2,1,16,128]{4,3,2,1,0:T(8,128)S(1)} fusion(bf16[32,2,2,16,128]{4,3,2,1,0:T(8,128)(2,1)} %get-tuple-element.10), kind=kLoop, calls=%fused_computation.9 | loop fusion | flops 131072 | bytes 786432 | tf_op jit(solution)/shard_map/convert_element_type | solution.py:314
  57.5 0.0 copy-done.5
  57.5 0.0 copy-done.6
  57.5 0.0 copy-done
  57.5 0.0 copy-done.3
  57.5 0.0 copy-done.4
  57.5 0.0 copy-start.2
  57.5 1.0 %fusion.2 = (bf16[32,32,128]{2,1,0:T(8,128)(2,1)}, bf16[32,32,128]{2,1,0:T(8,128)(2,1)}) fusion(bf16[32,32,128]{2,1,0:T(8,128)(2,1)S(1)} %copy-done.3, bf16[32,32,128]{2,1,0:T(8,128)(2,1)S(1)} %copy-done.4, f32[128]{0:T(128)S(1)} %bitcast.29, f32[128]{0:T(128)S(1)} %bitcast.27, bf16[32,32,128]{2,1,0:T(8,128)(2,1)S(1)} %bitcast.19, ...), kind=kLoop, calls=%fused_computation.4 | loop fusion | flops 1310720 | bytes 1836032 | tf_op jit(solution)/shard_map/convert_element_type | solution.py:315
  58.5 0.1 copy-done.2
  58.6 0.0 copy-start.1
  58.6 0.9 %convert_multiply_fusion.1 = f32[32,2,1,16,128]{4,3,2,1,0:T(8,128)} fusion(bf16[32,2,2,16,128]{4,3,2,1,0:T(8,128)(2,1)S(1)} %copy-done.2), kind=kLoop, calls=%fused_computation.7 | loop fusion | flops 262144 | bytes 786432 | tf_op jit(solution)/shard_map/div | solution.py:318
  59.4 0.1 copy-done.1
  59.5 0.8 %multiply_convert_fusion = bf16[1,1,1024,128]{3,2,1,0:T(8,128)(2,1)} fusion(f32[1,1,1024,128]{3,2,1,0:T(8,128)S(1)} %bitcast.17, bf16[1,1,1024,128]{3,2,1,0:T(8,128)(2,1)S(1)} %copy-done.1, f32[128]{0:T(128)S(1)} %bitcast.28), kind=kLoop, calls=%fused_computation.8 | loop fusion | flops 524288 | bytes 1049088 | tf_op jit(solution)/shard_map/convert_element_type | solution.py:316
Async XLA Ops:
  56.3 1.1 %copy-start.5 = (f32[1,128]{1,0:T(1,128)S(1)}, f32[1,128]{1,0:T(1,128)}, u32[]{:S(2)}) copy-start(f32[1,128]{1,0:T(1,128)} %get-tuple-element.11) | copy-start | bytes 1540
  56.3 1.1 %copy-start.6 = (f32[1,128]{1,0:T(1,128)S(1)}, f32[1,128]{1,0:T(1,128)}, u32[]{:S(2)}) copy-start(f32[1,128]{1,0:T(1,128)} %get-tuple-element.12) | copy-start | bytes 1540
  56.3 1.1 %copy-start = (bf16[1,1,1024,128]{3,2,1,0:T(8,128)(2,1)S(1)}, bf16[1,1,1024,128]{3,2,1,0:T(8,128)(2,1)}, u32[]{:S(2)}) copy-start(bf16[1,1,1024,128]{3,2,1,0:T(8,128)(2,1)} %param.14) | copy-start | bytes 786436
  56.4 1.1 %copy-start.3 = (bf16[32,32,128]{2,1,0:T(8,128)(2,1)S(1)}, bf16[32,32,128]{2,1,0:T(8,128)(2,1)}, u32[]{:S(2)}) copy-start(bf16[32,32,128]{2,1,0:T(8,128)(2,1)} %get-tuple-element.9) | copy-start | bytes 786436
  56.4 1.2 %copy-start.4 = (bf16[32,32,128]{2,1,0:T(8,128)(2,1)S(1)}, bf16[32,32,128]{2,1,0:T(8,128)(2,1)}, u32[]{:S(2)}) copy-start(bf16[32,32,128]{2,1,0:T(8,128)(2,1)} %get-tuple-element.13) | copy-start | bytes 786436
  57.5 1.0 %copy-start.2 = (bf16[32,2,2,16,128]{4,3,2,1,0:T(8,128)(2,1)S(1)}, bf16[32,2,2,16,128]{4,3,2,1,0:T(8,128)(2,1)}, u32[]{:S(2)}) copy-start(bf16[32,2,2,16,128]{4,3,2,1,0:T(8,128)(2,1)} %get-tuple-element.10) | copy-start | bytes 1572868
  58.6 0.9 %copy-start.1 = (bf16[1,1,1024,128]{3,2,1,0:T(8,128)(2,1)S(1)}, bf16[1,1,1024,128]{3,2,1,0:T(8,128)(2,1)}, u32[]{:S(2)}) copy-start(bf16[1,1,1024,128]{3,2,1,0:T(8,128)(2,1)} %param.15) | copy-start | bytes 786436

commit v5 on v4

--- a/solution.py
+++ b/solution.py
@@ -112,6 +112,7 @@
 
 MESH = pl.DeviceIdType.MESH
 PIECES = 2
+STRIDE = 13
 OUTWARD, CONV, GRAD, BACK = 0, 1, 2, 2 + PIECES
 STREAMS = 2 + 2 * PIECES
 LOADS = 9
@@ -120,8 +121,8 @@
 def kernel(
     docs_ref, layers_ref, handed_ref, gate_home, key_home, input_home, filter_ref,
     spread_home, gather_home, ahead_home, back_home, turns_home,
-    incoming_ref, conv_ref, both_ref, live_ref, scale_ref,
-    first_out, first_wide, grad_out, grad_wide, conv_wide, both_wide,
+    incoming_ref, conv_ref, corr_ref, lag_ref, live_ref, scale_ref,
+    first_out, first_wide, grad_out, grad_wide, conv_wide, both_wide, both_ref,
     filter_spec, prod_spec, grad_spec,
     gate_ref, key_ref, input_ref, spread_ref, gather_ref, ahead_ref, back_ref, turns_ref,
     send_sems, recv_sems, relay_send, relay_recv, load_sems,
@@ -152,7 +153,7 @@
 
     def scatter(source, target, stream):
         def step(index, carry):
-            peer = lax.rem(me + index, blocks)
+            peer = lax.rem(me + STRIDE * index, blocks)
             pltpu.make_async_remote_copy(
                 src_ref=source.at[peer],
                 dst_ref=target.at[me],
@@ -264,6 +265,9 @@
         relay(piece).wait_send()
         settle(part(grad_wide, piece), GRAD + piece).wait_send()
         settle(both_ref.at[:, piece], BACK + piece).wait()
+        span = pl.ds(share * piece, share)
+        corr_ref[:, span, :] = both_ref[:, piece, 0]
+        lag_ref[:, span, :] = both_ref[:, piece, 1]
 
 
 def mixer(docs, layers, handed, gate, key, inputs, filters):
@@ -280,10 +284,11 @@
     fixed = tables(blocks, width)
     return pl.pallas_call(
         kernel,
-        out_shape=(moved, moved, jax.ShapeDtypeStruct(both, jnp.bfloat16), line, line),
+        out_shape=(moved, moved, moved, moved, line, line),
         in_specs=[small] * 2 + [far] * 10,
-        out_specs=(held,) * 5,
-        scratch_shapes=[double, double, wide, wide, wide, pltpu.VMEM(both, jnp.bfloat16)]
+        out_specs=(held,) * 6,
+        scratch_shapes=[double, double, wide, wide, wide]
+        + [pltpu.VMEM(both, jnp.bfloat16)] * 2
         + [spec] * 3
         + [wide] * 3
         + [pltpu.VMEM(table.shape, table.dtype) for table in fixed]
@@ -305,8 +310,7 @@
     blocks = lax.axis_size("ctx")
     shape = (blocks, channels // blocks, width)
     blocked = [v.reshape(shape) for v in (handed_back, gate_q, key_k, input_x, filter_h)]
-    incoming, conv, both, live, scale = mixer(doc_lengths, section_layers, *blocked)
-    corr, lags = [both[:, :, i].reshape(shape) for i in range(2)]
+    incoming, conv, corr, lags, live, scale = mixer(doc_lengths, section_layers, *blocked)
     live, scale = live[None], scale[None]
     key32 = blocked[2].astype(jnp.float32)
     input32 = blocked[3].astype(jnp.float32)

time: 60.6 us -> 59.7 us (0.985)
  other arithmetic: 3.67 us -> 2.54 us
    convert_element_type x2 -> x0, other arithmetic: 2.03 us -> none  [the longest x1 1.07 us: body(): corr32 = corr.astype(jnp.float32)]
    convert_element_type x1, other arithmetic: 0.78 us -> 2.54 us  [body(): grad_key = (corr32 * input32 * live).astype(jnp.bfloat16)]
    div x1 -> x0, other arithmetic: 0.86 us -> none  [body(): grad_filter = lags.astype(jnp.float32) / math.sqrt(blocks * width)]
where the time goes in v5:
time: 59.7 us; the launch traced here: 59.5 us
  Pallas kernels  55.6 us (93%)
  other arithmetic  2.54 us (4%)
  between operations  0.69 us (1%)
  local copies, waits for them, and re-layouts  0.64 us (1%)
    pallas_call x1, Pallas kernels, mixer(): pl.pallas_call(kernel, out_shape=(moved, moved, moved, moved, line, line)...  55.6 us
    convert_element_type x1, other arithmetic, body(): grad_key = (corr32 * input32 * live).astype(jnp.bfloat16)  2.54 us

profile of v5, /device:TPU:1, one launch (start us, length us, event | category | flops | bytes accessed | tf_op | source)
XLA Modules:
  0.0 59.5 jit_solution(17177403825290038854)
XLA Ops:
  0.6 0.0 copy-start
  0.6 0.0 copy-start.1
  0.7 55.6 %shard_map.147 = (bf16[32,32,128]{2,1,0:T(8,128)(2,1)}, bf16[32,32,128]{2,1,0:T(8,128)(2,1)}, bf16[32,32,128]{2,1,0:T(8,128)(2,1)}, bf16[32,32,128]{2,1,0:T(8,12...) custom-call(s32[1,8]{1,0:T(1,128)} %docs_ref.1, s32[4]{0:T(128)} %layers_ref.1, bf16[32,32,128]{2,1,0:T(8,128)(2,1)} %bitcast.16, ...), custom_call_target="tpu_custom_call" | custom-call | tf_op jit(solution)/shard_map/pallas_call | solution.py:285
  56.3 0.0 copy-start.2
  56.3 0.0 copy-start.3
  56.3 0.0 copy-done
  56.3 0.0 copy-done.1
  56.3 0.6 %copy-done.2 = f32[1,128]{1,0:T(1,128)S(1)} copy-done((f32[1,128]{1,0:T(1,128)S(1)}, f32[1,128]{1,0:T(1,128)}, u32[]{:S(2)}) %copy-start.2) | copy-done | bytes 536
  57.0 0.0 copy-done.3
  57.0 2.5 %fusion.5 = (bf16[32,32,128]{2,1,0:T(8,128)(2,1)}, bf16[32,32,128]{2,1,0:T(8,128)(2,1)}, bf16[32,32,128]{2,1,0:T(8,128)(2,1)}, f32[32,32,128]{2,1,0:T(8,128)}) fusion(bf16[32,32,128]{2,1,0:T(8,128)(2,1)} %get-tuple-element.11, bf16[32,32,128]{2,1,0:T(8,128)(2,1)S(1)} %bitcast.14, f32[128]{0:T(128)S(1)} %bitcast.22, bf16[32,32,128]{2,1,0:T(8,128)(2,1)S(1)} %bitcast.12, ...), kind=kLoop, calls=%fused_computation.9 | loop fusion | flops 2228224 | bytes 2884608 | tf_op jit(solution)/shard_map/convert_element_type | solution.py:320
Async XLA Ops:
  0.6 55.7 %copy-start = (bf16[1,1,1024,128]{3,2,1,0:T(8,128)(2,1)S(1)}, bf16[1,1,1024,128]{3,2,1,0:T(8,128)(2,1)}, u32[]{:S(2)}) copy-start(bf16[1,1,1024,128]{3,2,1,0:T(8,128)(2,1)} %param.14) | copy-start | bytes 786436
  0.6 55.7 %copy-start.1 = (bf16[1,1,1024,128]{3,2,1,0:T(8,128)(2,1)S(1)}, bf16[1,1,1024,128]{3,2,1,0:T(8,128)(2,1)}, u32[]{:S(2)}) copy-start(bf16[1,1,1024,128]{3,2,1,0:T(8,128)(2,1)} %param.15) | copy-start | bytes 786436
  56.3 0.7 %copy-start.2 = (f32[1,128]{1,0:T(1,128)S(1)}, f32[1,128]{1,0:T(1,128)}, u32[]{:S(2)}) copy-start(f32[1,128]{1,0:T(1,128)} %get-tuple-element.12) | copy-start | bytes 1540
  56.3 0.7 %copy-start.3 = (f32[1,128]{1,0:T(1,128)S(1)}, f32[1,128]{1,0:T(1,128)}, u32[]{:S(2)}) copy-start(f32[1,128]{1,0:T(1,128)} %get-tuple-element.13) | copy-start | bytes 1540
